TPU v7x, 256 devices: a whole 4x4x8 slice. The times are simulated.
256 devices in a mesh: ctx: 16 (over y, x), head: 4 (over z_hi, core), dp: 4 (over z_lo).
Axes of the slice: x: 4, y: 4, z: 8 (z_hi: 2, z_lo: 4; z = z_hi * 4 + z_lo), core: 2. Of those that a mesh axis runs over, the one named last changes fastest.
Arguments:
- queries: bfloat16 [4096, 8, 8, 128], P('ctx', 'head', 'dp'), may hold values from -2.5 to 2.5
- key_rows: bfloat16 [4096, 8, 128], P(('ctx', 'dp'), 'head'), may hold values from -2.5 to 2.5
- value_rows: bfloat16 [4096, 8, 128], P(('ctx', 'dp'), 'head'), may hold values from -6 to 6
- forward_out: bfloat16 [4096, 8, 8, 128], P('ctx', 'head', 'dp'), may hold values from -0.59765625 to 0.59765625
- grad_out: bfloat16 [4096, 8, 8, 128], P('ctx', 'head', 'dp'), may hold values from -24 to 24
- logsumexp: float32 [8, 8, 4096], P('head', 'dp', 'ctx'), as said below
- selected: int32 [16, 8, 8, 8], P('ctx', 'head', 'dp'), may hold values from -1 to 15, as said below
Outputs:
- query_grad: bfloat16 [4096, 8, 8, 128], P('ctx', 'head', 'dp')
- key_grad: float32 [4096, 8, 128], P(('ctx', 'dp'), 'head')
- value_grad: float32 [4096, 8, 128], P(('ctx', 'dp'), 'head')
Inputs may be any that keep to these rules, and one draw needn't show every extreme that they name: selected[i, a, g, 0] = i. The other entries of a row are distinct blocks below i (some blocks below i may be left out), followed by -1 in the slots that remain. `logsumexp`: each entry lies between log(512) and log(512) + 1.5.
All inputs are finite; a program needn't handle non-finite values.
Results may differ from a plain program's by a relative error of at most 0.0051.
Values may be sent and summed in bfloat16 or wider, within the bound.
No kernel may reach another device: no remote copies, remote signals or barrier semaphores. Data moves between devices by JAX's collectives and lax.ppermute only.
A program may use at most 64 MiB of HBM per device.

v0:
```python
import jax
import jax.numpy as jnp
from jax import lax
from jax.experimental import pallas as pl
from jax.experimental.pallas import tpu as pltpu
from jax.sharding import PartitionSpec as P


BLOCK = 256
SIDE = 4


def shifts(rows, columns):
    return [
        (y * SIDE + x, (y + rows) % SIDE * SIDE + (x + columns) % SIDE)
        for y in range(SIDE)
        for x in range(SIDE)
    ]


def move(array, rows, columns):
    return lax.ppermute(array, "ctx", shifts(rows, columns))


def swap(array, bit):
    return lax.ppermute(array, "dp", [(d, d ^ bit) for d in range(4)])


def gather_small(own, rows, columns):
    before = move(own, rows, columns)
    after = move(own, -rows, -columns)
    far = move(own, 2 * rows, 2 * columns)
    return jnp.stack([own, before, far, after])


def gather_large(own, rows, columns):
    before = move(own, rows, columns)
    after = move(own, -rows, -columns)
    far = move(before, rows, columns)
    return own, before, after, far


def reduce_large(own, before, after, far, rows, columns):
    full = jnp.float32
    after = move(after, rows, columns)
    far, own = lax.optimization_barrier((move(far, -rows, -columns), own))
    before = move((before.astype(full) + far.astype(full)).astype(before.dtype), -rows, -columns)
    return own + before.astype(full) + after.astype(full)


def reduce_small(terms, rows, columns):
    full, low = jnp.float32, terms.astype(jnp.bfloat16)
    far = move(low[2], -2 * rows, -2 * columns)
    before = move(low[1], -rows, -columns)
    after = move(low[3], rows, columns)
    return terms[0] + far.astype(full) + before.astype(full) + after.astype(full)


SETS, WORDS, ROOM = 3, 6, 40
NONE = -2 * BLOCK


def plan(sel, place, qd_own, qd_far, table, qd, count, *, pairs):
    for half, part in enumerate((qd_own, qd_far)):
        for g in range(pairs // 2):
            for n in range(2):
                qd[n, half * (pairs // 2) + g] = part[n, g]
    row, column = place[0], place[1]

    def put(c, word, at, value):
        table[(c * WORDS + word) * ROOM + at] = jnp.int32(value)

    for c in range(SETS):
        count[c] = 0
    for pair in range(pairs):
        for s in range(sel.shape[1]):
            block = sel[pair, s]
            y, x = (block >> 2) & 3, block & 3
            if (pair >> 1) & 1 == 0:
                distance, other = (row - y) & 3, (column - x) & 3
            else:
                distance, other = (column - x) & 3, (row - y) & 3
            c = jnp.where(distance == 0, 2, jnp.where(distance == 2, 1, 0))
            at = count[c]
            word = (at & 1) * 2
            put(c, 0, at >> 1, pair)
            put(c, word + 1, at >> 1, other + jnp.where(distance == 3, SIDE, 0))
            put(c, word + 2, at >> 1, 0 if s == 0 else BLOCK)
            count[c] = at + (block >= 0).astype(jnp.int32)
        for c in range(SETS):
            at = count[c]
            put(c, 3, at >> 1, 0)
            put(c, 4, at >> 1, NONE)
            count[c] = at + (at & 1)
    for c in range(SETS):
        at = count[c] >> 1
        for word, value in enumerate((0, 0, NONE, 0, NONE)):
            put(c, word, at, value)
        put(c, 5, 0, at)


def plan_call(sel, place, qd_own, qd_far):
    vmem = pl.BlockSpec(memory_space=pltpu.VMEM)
    smem = pl.BlockSpec(memory_space=pltpu.SMEM)
    pairs = sel.shape[0]
    shape = (2, pairs) + qd_own.shape[2:]
    return pl.pallas_call(
        lambda *refs: plan(*refs, pairs=pairs),
        out_shape=[
            jax.ShapeDtypeStruct((SETS * WORDS * ROOM,), jnp.int32),
            jax.ShapeDtypeStruct(shape, qd_own.dtype),
        ],
        in_specs=[smem, smem, vmem, vmem],
        out_specs=[smem, vmem],
        scratch_shapes=[pltpu.SMEM((SETS + 1,), jnp.int32)],
        name="plan",
        compiler_params=pltpu.CompilerParams(vmem_limit_bytes=8 << 20),
        cost_estimate=pl.CostEstimate(flops=1 << 20, bytes_accessed=4 << 20, transcendentals=0),
    )(sel, place, qd_own, qd_far)


def attend(table, place, stats, qd, *refs, which, parts, scale, pairs, first, final):
    half_rows = BLOCK // 2
    half_pairs = pairs // 2
    low, full = jnp.bfloat16, jnp.float32
    given = refs[: 2 * parts]
    refs = refs[2 * parts :]
    if not first:
        dq_in, refs = refs[0], refs[1:]
    terms, refs = refs[: 2 * parts], refs[2 * parts :]
    if final:
        dq_own, dq_far, dq_t = refs[0], refs[1], refs[-1]
        rows, acc, p_even, s_even, p_odd, s_odd = refs[2:-1]
    else:
        dq_t = refs[0]
        rows, acc, p_even, s_even, p_odd, s_odd = refs[1:]
    blocks = parts * SIDE

    def word(n, at):
        return table[(which * WORDS + n) * ROOM + at]

    total = word(5, 0)
    if first:
        dq_t[...] = jnp.zeros_like(dq_t)
    else:
        dq_t[...] = dq_in[...]

    def slot(head, n, r):
        return (head * blocks + n * SIDE + r) * 2

    for head in range(2):
        for n in range(parts):
            for r in range(SIDE):
                for kv in range(2):
                    at = slot(head, n, r) + kv
                    rows[at] = given[head * parts + n][r, kv * half_rows : (kv + 1) * half_rows]
                    acc[at] = jnp.zeros(acc.shape[1:], full)

    at_row = lax.broadcasted_iota(jnp.int32, (half_rows, BLOCK), 0)
    at_query = lax.broadcasted_iota(jnp.int32, (half_rows, BLOCK), 1)
    quarter = BLOCK // 4
    offset = at_row + place[2] * quarter + jnp.where(at_row >= quarter, quarter, 0) - at_query

    def across(one, two, dim):
        return lax.dot_general(one, two, (((dim,), (dim,)), ((), ())), preferred_element_type=full)

    def item(n):
        pair = word(0, n)
        base = ((pair >> 1) & 1) * blocks
        return pair, (base + word(1, n)) * 2, (base + word(3, n)) * 2

    def weigh(n, p_buf, s_buf):
        pair, one, two = item(n)
        lse = stats[pl.ds(pair, 1), :]
        delta = stats[pl.ds(pair + pairs, 1), :]
        k = jnp.concatenate([rows[one], rows[two]], axis=0)
        scores = across(k, qd[0, pair], 1) * scale
        keep = jnp.concatenate([offset <= word(2, n), offset <= word(4, n)], axis=0)
        probs = jnp.where(keep, jnp.exp(scores - lse), 0.0)
        p_buf[...] = probs.astype(low)
        v = jnp.concatenate([rows[one + 1], rows[two + 1]], axis=0)
        dprobs = across(v, qd[1, pair], 1)
        s_buf[...] = (probs * (dprobs - delta) * scale).astype(low)

    def spread(n, p_buf, s_buf):
        pair, one, two = item(n)
        dv = jnp.dot(p_buf[...], qd[1, pair], preferred_element_type=full)
        acc[one + 1] += dv[:half_rows]
        acc[two + 1] += dv[half_rows:]
        dk = jnp.dot(s_buf[...], qd[0, pair], preferred_element_type=full)
        acc[one] += dk[:half_rows]
        acc[two] += dk[half_rows:]
        k = jnp.concatenate([rows[one], rows[two]], axis=0)
        dq_t[pair] += across(k, s_buf[...], 0)

    @pl.when(total > 0)
    def _():
        weigh(0, p_even, s_even)
        steps = (total + 1) >> 1

        @pl.loop(0, steps - 1)
        def _(i):
            weigh(2 * i + 1, p_odd, s_odd)
            spread(2 * i, p_even, s_even)
            weigh(2 * i + 2, p_even, s_even)
            spread(2 * i + 1, p_odd, s_odd)

        last = 2 * steps - 2
        weigh(last + 1, p_odd, s_odd)
        spread(last, p_even, s_even)
        spread(last + 1, p_odd, s_odd)

    for head in range(2):
        for n in range(parts):
            out = terms[head * parts + n]
            for r in range(SIDE):
                for kv in range(2):
                    out[r, kv * half_rows : (kv + 1) * half_rows] = acc[slot(head, n, r) + kv].astype(
                        out.dtype
                    )
    if final:
        for g in range(half_pairs):
            dq_own[g] = dq_t[g].T
            dq_far[g] = dq_t[half_pairs + g].T.astype(low)


def attend_call(which, table, place, stats, qd, given, dq, final):
    low, full = jnp.bfloat16, jnp.float32
    vmem = pl.BlockSpec(memory_space=pltpu.VMEM)
    smem = pl.BlockSpec(memory_space=pltpu.SMEM)
    parts = len(given) // 2
    pairs, head_dim = qd.shape[1], qd.shape[-1]
    first = dq is None
    share = 8 * parts
    term = jax.ShapeDtypeStruct(given[0].shape, full if final else low)
    dq_shape = jax.ShapeDtypeStruct((pairs, head_dim, BLOCK), full)
    if final:
        dq_outs = [
            jax.ShapeDtypeStruct((pairs // 2, BLOCK, head_dim), full),
            jax.ShapeDtypeStruct((pairs // 2, BLOCK, head_dim), low),
        ]
    else:
        dq_outs = [dq_shape]
    held = parts * SIDE * 4
    square = pltpu.VMEM((BLOCK, BLOCK), low)
    scratch = [
        pltpu.VMEM((held, BLOCK // 2, head_dim), low),
        pltpu.VMEM((held, BLOCK // 2, head_dim), full),
        square,
        square,
        square,
        square,
    ]
    if final:
        scratch.append(pltpu.VMEM((pairs, head_dim, BLOCK), full))
    operands = (table, place, stats, qd, *given) + (() if first else (dq,))
    outs = pl.pallas_call(
        lambda *refs: attend(
            *refs,
            which=which,
            parts=parts,
            scale=head_dim**-0.5,
            pairs=pairs,
            first=first,
            final=final,
        ),
        out_shape=[term] * len(given) + dq_outs,
        in_specs=[smem, smem] + [vmem] * (len(operands) - 2),
        out_specs=[vmem] * (len(given) + len(dq_outs)),
        scratch_shapes=scratch,
        compiler_params=pltpu.CompilerParams(vmem_limit_bytes=20 << 20),
        cost_estimate=pl.CostEstimate(
            flops=share * 5 * 2 * BLOCK * BLOCK * head_dim,
            bytes_accessed=(2 * parts + 4) << 20,
            transcendentals=share * BLOCK * BLOCK,
        ),
    )(*operands)
    return outs[: len(given)], outs[len(given) :]


def step(queries, key_rows, value_rows, forward_out, grad_out, logsumexp, selected):
    rows, heads, members, head_dim = queries.shape
    pairs = heads * members
    low, full = jnp.bfloat16, jnp.float32
    ctx, dp = lax.axis_index("ctx"), lax.axis_index("dp")
    lower = dp < 2

    kv = jnp.stack([key_rows, value_rows]).transpose(2, 0, 1, 3)
    far = swap(kv, 2)
    kv = jnp.where(lower, jnp.concatenate([kv, far], 2), jnp.concatenate([far, kv], 2))
    kv = kv.reshape(heads, BLOCK, head_dim)

    qd_own = jnp.stack([queries, grad_out]).transpose(0, 2, 3, 1, 4).reshape(2, pairs, rows, head_dim)
    qd_far = swap(qd_own, 1)

    own_0, before_0, after_0, far_0 = gather_large(gather_small(kv[0], 0, 1), 1, 0)
    own_1, before_1, after_1, far_1 = gather_large(gather_small(kv[1], 1, 0), 0, 1)

    delta = jnp.sum(grad_out.astype(full) * forward_out.astype(full), axis=-1).transpose(1, 2, 0)
    ids = jnp.pad(selected[0].astype(full), ((0, 0), (0, 0), (0, BLOCK - selected.shape[-1])))
    small = jnp.stack([logsumexp, delta, ids]).reshape(3, pairs, BLOCK)
    small_far = swap(small, 1)
    small = jnp.concatenate([small, small_far], axis=1)
    stats = small[0:2].reshape(4 * pairs, BLOCK)
    sel = small[2, :, : selected.shape[-1]].astype(jnp.int32)
    place = jnp.stack([ctx // SIDE, ctx % SIDE, dp % 2]).astype(jnp.int32)

    table, qd = plan_call(sel, place, qd_own, qd_far)
    shared = (table, place, stats, qd)
    near_parts = (before_0, after_0, before_1, after_1)
    (before_0, after_0, before_1, after_1), (dq,) = attend_call(0, *shared, near_parts, None, False)
    (far_0, far_1), (dq,) = attend_call(1, *shared, (far_0, far_1), dq, False)
    (own_0, own_1), (dq_own, dq_far) = attend_call(2, *shared, (own_0, own_1), dq, True)

    query_grad = (dq_own + swap(dq_far, 1).astype(full)).astype(low)
    query_grad = query_grad.reshape(heads, members, rows, head_dim).transpose(2, 0, 1, 3)

    grad_0 = reduce_small(reduce_large(own_0, before_0, after_0, far_0, 1, 0), 0, 1)
    grad_1 = reduce_small(reduce_large(own_1, before_1, after_1, far_1, 0, 1), 1, 0)

    grads = jnp.stack([grad_0, grad_1]).reshape(heads, 2, 2, BLOCK // 4, head_dim)
    keep = jnp.where(lower, grads[:, :, 0], grads[:, :, 1])
    send = jnp.where(lower, grads[:, :, 1], grads[:, :, 0]).astype(low)
    grads = (keep + swap(send, 2).astype(full)).transpose(1, 2, 0, 3)
    return (query_grad, grads[0], grads[1])


def solution(mesh):
    return jax.shard_map(
        step,
        mesh=mesh,
        in_specs=(
            P("ctx", "head", "dp", None),
            P(("ctx", "dp"), "head", None),
            P(("ctx", "dp"), "head", None),
            P("ctx", "head", "dp", None),
            P("ctx", "head", "dp", None),
            P("head", "dp", "ctx"),
            P("ctx", "head", "dp", None),
        ),
        out_specs=(
            P("ctx", "head", "dp", None),
            P(("ctx", "dp"), "head", None),
            P(("ctx", "dp"), "head", None),
        ),
        check_vma=False,
    )
```

profile of v0, /device:TPU:0, one launch (start us, length us, event | category | flops | bytes accessed | tf_op | source)
XLA Modules:
  0.0 82.8 jit_solution(12229106713565512849)
XLA Ops:
  1.5 1.6 %collective-permute-start.2 = (bf16[2,2,64,128]{3,2,1,0:T(8,128)(2,1)S(1)}, bf16[2,2,64,128]{3,2,1,0:T(8,128)(2,1)S(1)}, u32[]{:S(2)}, u32[]{:S(2)}) collective-permute-start(bf16[2,2,64,128]{3,2,1,0:T(8,128)(2,1)S(1)} %maximum_bitcast_fusion.1), channel_id=1, source_target_pairs={{0,2},{1,3},{2,0},{3,1},{4,6},{5,7},{6,4},{7,5},{8,10},{9,11},{10,... | collective-permute-start | bytes 196616 | tf_op jit(solution)/shard_map/ppermute | solution.py:26
  3.1 1.7 %maximum_bitcast_fusion = bf16[2,2,2,256,128]{4,2,1,3,0:T(2,128)(2,1)S(1)} fusion(bf16[1,256,2,2,128]{4,3,2,1,0:T(2,128)(2,1)S(1)} %bitcast.80, bf16[1,256,2,2,128]{4,3,2,1,0:T(2,128)(2,1)} %bitcast.85), kind=kLoop, calls=%fused_computation | loop fusion | flops 262144 | bytes 1048576 | tf_op jit(solution)/shard_map/transpose | solution.py:293
  5.0 2.0 %collective-permute-start.1 = (bf16[2,4,256,128]{3,2,1,0:T(8,128)(2,1)S(1)}, bf16[2,4,256,128]{3,2,1,0:T(8,128)(2,1)S(1)}, u32[]{:S(2)}, u32[]{:S(2)}) collective-permute-start(bf16[2,4,256,128]{3,2,1,0:T(8,128)(2,1)S(1)} %bitcast.77), channel_id=1, source_target_pairs={{0,1},{1,0},{2,3},{3,2},{4,5},{5,4},{6,7},{7,6},{8,9},{9,8},{10,11... | collective-permute-start | bytes 1572872 | tf_op jit(solution)/shard_map/ppermute | solution.py:26
  8.8 3.1 %collective-permute-start.8 = (bf16[256,128]{1,0:T(8,128)(2,1)S(1)}, bf16[256,128]{1,0:T(8,128)(2,1)S(1)}, u32[]{:S(2)}, u32[]{:S(2)}) collective-permute-start(bf16[256,128]{1,0:T(8,128)(2,1)S(1)} %bitcast.90), channel_id=1, source_target_pairs={{0,192},{16,208},{32,224},{48,240},{64,0},{80,16},{96,32},{112,48}... | collective-permute-start | bytes 196616 | tf_op jit(solution)/shard_map/ppermute | solution.py:22
  13.5 2.8 %collective-permute-start.5 = (bf16[256,128]{1,0:T(8,128)(2,1)S(1)}, bf16[256,128]{1,0:T(8,128)(2,1)S(1)}, u32[]{:S(2)}, u32[]{:S(2)}) collective-permute-start(bf16[256,128]{1,0:T(8,128)(2,1)S(1)} %bitcast.86), channel_id=1, source_target_pairs={{0,48},{16,0},{32,16},{48,32},{64,112},{80,64},{96,80},{112,96},{1... | collective-permute-start | bytes 196616 | tf_op jit(solution)/shard_map/ppermute | solution.py:22
  17.7 1.5 %collective-permute-start.3 = (bf16[256,128]{1,0:T(8,128)(2,1)S(1)}, bf16[256,128]{1,0:T(8,128)(2,1)S(1)}, u32[]{:S(2)}, u32[]{:S(2)}) collective-permute-start(bf16[256,128]{1,0:T(8,128)(2,1)S(1)} %bitcast.88), channel_id=1, source_target_pairs={{0,16},{16,32},{32,48},{48,0},{64,80},{80,96},{96,112},{112,64},{1... | collective-permute-start | bytes 196616 | tf_op jit(solution)/shard_map/ppermute | solution.py:22
  19.2 1.6 %collective-permute-start.11 = (bf16[4,256,128]{2,1,0:T(8,128)(2,1)S(1)}, bf16[4,256,128]{2,1,0:T(8,128)(2,1)S(1)}, u32[]{:S(2)}, u32[]{:S(2)}) collective-permute-start(bf16[4,256,128]{2,1,0:T(8,128)(2,1)S(1)} %pad_maximum_fusion.1.refs_5_), channel_id=1, source_target_pairs={{0,16},{16,32},{32,48},{48,0},{64,80},{80,96},{96,112},{112,64},{1... | collective-permute-start | bytes 786440 | tf_op jit(solution)/shard_map/ppermute | solution.py:22
  20.8 1.9 %collective-permute-done.4 = bf16[256,128]{1,0:T(8,128)(2,1)S(1)} collective-permute-done((bf16[256,128]{1,0:T(8,128)(2,1)S(1)}, bf16[256,128]{1,0:T(8,128)(2,1)S(1)}, u32[]{:S(2)}, u32[]{:S(2)}) %collective-permute-start.4) | collective-permute-done | bytes 65568 | tf_op jit(solution)/shard_map/ppermute | solution.py:22
  22.7 1.3 %collective-permute-done.3 = bf16[256,128]{1,0:T(8,128)(2,1)S(1)} collective-permute-done((bf16[256,128]{1,0:T(8,128)(2,1)S(1)}, bf16[256,128]{1,0:T(8,128)(2,1)S(1)}, u32[]{:S(2)}, u32[]{:S(2)}) %collective-permute-start.3) | collective-permute-done | bytes 65568 | tf_op jit(solution)/shard_map/ppermute | solution.py:22
  24.0 1.6 %collective-permute-start.9 = (bf16[4,256,128]{2,1,0:T(8,128)(2,1)S(1)}, bf16[4,256,128]{2,1,0:T(8,128)(2,1)S(1)}, u32[]{:S(2)}, u32[]{:S(2)}) collective-permute-start(bf16[4,256,128]{2,1,0:T(8,128)(2,1)S(1)} %pad_maximum_fusion.refs_4_), channel_id=1, source_target_pairs={{0,64},{16,80},{32,96},{48,112},{64,128},{80,144},{96,160},{112,17... | collective-permute-start | bytes 786440 | tf_op jit(solution)/shard_map/ppermute | solution.py:22
  26.5 1.0 %collective-permute-start.14 = (bf16[4,256,128]{2,1,0:T(8,128)(2,1)S(1)}, bf16[4,256,128]{2,1,0:T(8,128)(2,1)S(1)}, u32[]{:S(2)}, u32[]{:S(2)}) collective-permute-start(bf16[4,256,128]{2,1,0:T(8,128)(2,1)S(1)} %pad_maximum_fusion.1.refs_5_), channel_id=1, source_target_pairs={{0,48},{16,0},{32,16},{48,32},{64,112},{80,64},{96,80},{112,96},{1... | collective-permute-start | bytes 786440 | tf_op jit(solution)/shard_map/ppermute | solution.py:22
  27.6 1.9 %collective-permute-done = f32[3,4,256]{2,1,0:T(4,128)S(1)} collective-permute-done((f32[3,4,256]{2,1,0:T(4,128)S(1)}, f32[3,4,256]{2,1,0:T(4,128)S(1)}, u32[]{:S(2)}, u32[]{:S(2)}) %collective-permute-start) | collective-permute-done | bytes 12320 | tf_op jit(solution)/shard_map/ppermute | solution.py:26
  29.5 1.7 %collective-permute-start.13 = (bf16[4,256,128]{2,1,0:T(8,128)(2,1)S(1)}, bf16[4,256,128]{2,1,0:T(8,128)(2,1)S(1)}, u32[]{:S(2)}, u32[]{:S(2)}) collective-permute-start(bf16[4,256,128]{2,1,0:T(8,128)(2,1)S(1)} %pad_maximum_fusion.refs_4_), channel_id=1, source_target_pairs={{0,192},{16,208},{32,224},{48,240},{64,0},{80,16},{96,32},{112,48}... | collective-permute-start | bytes 786440 | tf_op jit(solution)/shard_map/ppermute | solution.py:22
  31.4 1.4 %collective-permute-done.9.refs_4_ = bf16[4,256,128]{2,1,0:T(8,128)(2,1)S(1)} collective-permute-done((bf16[4,256,128]{2,1,0:T(8,128)(2,1)S(1)}, bf16[4,256,128]{2,1,0:T(8,128)(2,1)S(1)}, u32[]{:S(2)}, u32[]{:S(2)}) %collective-permute-start.9) | collective-permute-done | bytes 262176 | tf_op jit(solution)/shard_map/ppermute | solution.py:22
  32.8 1.4 %collective-permute-start.10 = (bf16[4,256,128]{2,1,0:T(8,128)(2,1)S(1)}, bf16[4,256,128]{2,1,0:T(8,128)(2,1)S(1)}, u32[]{:S(2)}, u32[]{:S(2)}) collective-permute-start(bf16[4,256,128]{2,1,0:T(8,128)(2,1)S(1)} %collective-permute-done.9.refs_4_), channel_id=1, source_target_pairs={{0,64},{16,80},{32,96},{48,112},{64,128},{80,144},{96,160},{112,17... | collective-permute-start | bytes 786440 | tf_op jit(solution)/shard_map/ppermute | solution.py:22
  34.3 2.0 %plan.1 = (s32[720]{0:T(1024)S(1)}, bf16[2,8,256,128]{3,2,1,0:T(8,128)(2,1)S(1)}) custom-call(s32[8,8]{1,0:T(8,128)S(1)} %fusion.10.refs_0_, s32[3]{0:T(128)S(1)} %pad_add_fusion.refs_1_, bf16[2,4,256,128]{3,2,1,0:T(8,128)(2,1)S(1)} %bitcast.78, bf16[2,4,256,128]{3,2,1,0:T(8,128)(2,1)S(1)} %collective-permute-done.1.refs_3_), custom_call_target="tpu_custom_call" | custom-call | flops 1048576 | bytes 4194304 | tf_op jit(solution)/shard_map/plan/pallas_call | solution.py:107
  37.3 1.5 %collective-permute-done.12.refs_5_ = bf16[4,256,128]{2,1,0:T(8,128)(2,1)S(1)} collective-permute-done((bf16[4,256,128]{2,1,0:T(8,128)(2,1)S(1)}, bf16[4,256,128]{2,1,0:T(8,128)(2,1)S(1)}, u32[]{:S(2)}, u32[]{:S(2)}) %collective-permute-start.12) | collective-permute-done | bytes 262176 | tf_op jit(solution)/shard_map/ppermute | solution.py:22
  38.8 1.6 %collective-permute-done.10.refs_4_ = bf16[4,256,128]{2,1,0:T(8,128)(2,1)S(1)} collective-permute-done((bf16[4,256,128]{2,1,0:T(8,128)(2,1)S(1)}, bf16[4,256,128]{2,1,0:T(8,128)(2,1)S(1)}, u32[]{:S(2)}, u32[]{:S(2)}) %collective-permute-start.10) | collective-permute-done | bytes 262176 | tf_op jit(solution)/shard_map/ppermute | solution.py:22
  41.2 6.7 %collective-permute-start.16 = (bf16[4,256,128]{2,1,0:T(8,128)(2,1)S(1)}, bf16[4,256,128]{2,1,0:T(8,128)(2,1)S(1)}, u32[]{:S(2)}, u32[]{:S(2)}) collective-permute-start(bf16[4,256,128]{2,1,0:T(8,128)(2,1)S(1)} %get-tuple-element.27), channel_id=1, source_target_pairs={{0,192},{16,208},{32,224},{48,240},{64,0},{80,16},{96,32},{112,48}... | collective-permute-start | bytes 786440 | tf_op jit(solution)/shard_map/ppermute | solution.py:22
  47.9 1.4 %collective-permute-start.22 = (bf16[4,256,128]{2,1,0:T(8,128)(2,1)S(1)}, bf16[4,256,128]{2,1,0:T(8,128)(2,1)S(1)}, u32[]{:S(2)}, u32[]{:S(2)}) collective-permute-start(bf16[4,256,128]{2,1,0:T(8,128)(2,1)S(1)} %get-tuple-element.33), channel_id=1, source_target_pairs={{0,48},{16,0},{32,16},{48,32},{64,112},{80,64},{96,80},{112,96},{1... | collective-permute-start | bytes 786440 | tf_op jit(solution)/shard_map/ppermute | solution.py:22
  49.4 3.2 %shard_map.96 = (f32[4,256,128]{2,1,0:T(8,128)S(1)}, f32[4,256,128]{2,1,0:T(8,128)S(1)}, f32[4,256,128]{2,1,0:T(8,128)S(1)}, bf16[4,256,128]{2,1,0:T(8,128)(2,1)S(1)}) custom-call(s32[720]{0:T(1024)S(1)} %get-tuple-element.21.refs_0_, s32[3]{0:T(128)S(1)} %pad_add_fusion.refs_1_, f32[16,256]{1,0:T(8,128)S(1)} %fusion.9.refs_2_, ...), custom_call_target="tpu_custom_call" | custom-call | flops 671088640 | bytes 6291456 | tf_op jit(solution)/shard_map/pallas_call | solution.py:257
  53.5 3.8 %collective-permute-start.17 = (bf16[4,256,128]{2,1,0:T(8,128)(2,1)S(1)}, bf16[4,256,128]{2,1,0:T(8,128)(2,1)S(1)}, u32[]{:S(2)}, u32[]{:S(2)}) collective-permute-start(bf16[4,256,128]{2,1,0:T(8,128)(2,1)S(1)} %add_convert_fusion.1), channel_id=1, source_target_pairs={{0,192},{16,208},{32,224},{48,240},{64,0},{80,16},{96,32},{112,48}... | collective-permute-start | bytes 786440 | tf_op jit(solution)/shard_map/ppermute | solution.py:22
  57.9 3.2 %collective-permute-start.23 = (bf16[4,256,128]{2,1,0:T(8,128)(2,1)S(1)}, bf16[4,256,128]{2,1,0:T(8,128)(2,1)S(1)}, u32[]{:S(2)}, u32[]{:S(2)}) collective-permute-start(bf16[4,256,128]{2,1,0:T(8,128)(2,1)S(1)} %add_convert_fusion), channel_id=1, source_target_pairs={{0,48},{16,0},{32,16},{48,32},{64,112},{80,64},{96,80},{112,96},{1... | collective-permute-start | bytes 786440 | tf_op jit(solution)/shard_map/ppermute | solution.py:22
  61.2 2.4 %collective-permute-start.19 = (bf16[256,128]{1,0:T(8,128)(2,1)S(1)}, bf16[256,128]{1,0:T(8,128)(2,1)S(1)}, u32[]{:S(2)}, u32[]{:S(2)}) collective-permute-start(bf16[256,128]{1,0:T(8,128)(2,1)S(1)} %get-tuple-element.43), channel_id=1, source_target_pairs={{0,32},{16,48},{32,0},{48,16},{64,96},{80,112},{96,64},{112,80},{1... | collective-permute-start | bytes 196616 | tf_op jit(solution)/shard_map/ppermute | solution.py:22
  63.6 1.9 %collective-permute-start.21 = (bf16[256,128]{1,0:T(8,128)(2,1)S(1)}, bf16[256,128]{1,0:T(8,128)(2,1)S(1)}, u32[]{:S(2)}, u32[]{:S(2)}) collective-permute-start(bf16[256,128]{1,0:T(8,128)(2,1)S(1)} %get-tuple-element.44), channel_id=1, source_target_pairs={{0,16},{16,32},{32,48},{48,0},{64,80},{80,96},{96,112},{112,64},{1... | collective-permute-start | bytes 196616 | tf_op jit(solution)/shard_map/ppermute | solution.py:22
  65.5 1.3 %collective-permute-start.20 = (bf16[256,128]{1,0:T(8,128)(2,1)S(1)}, bf16[256,128]{1,0:T(8,128)(2,1)S(1)}, u32[]{:S(2)}, u32[]{:S(2)}) collective-permute-start(bf16[256,128]{1,0:T(8,128)(2,1)S(1)} %get-tuple-element.45), channel_id=1, source_target_pairs={{0,48},{16,0},{32,16},{48,32},{64,112},{80,64},{96,80},{112,96},{1... | collective-permute-start | bytes 196616 | tf_op jit(solution)/shard_map/ppermute | solution.py:22
  67.0 2.0 %collective-permute-start.25 = (bf16[256,128]{1,0:T(8,128)(2,1)S(1)}, bf16[256,128]{1,0:T(8,128)(2,1)S(1)}, u32[]{:S(2)}, u32[]{:S(2)}) collective-permute-start(bf16[256,128]{1,0:T(8,128)(2,1)S(1)} %get-tuple-element.46), channel_id=1, source_target_pairs={{0,128},{16,144},{32,160},{48,176},{64,192},{80,208},{96,224},{112... | collective-permute-start | bytes 196616 | tf_op jit(solution)/shard_map/ppermute | solution.py:22
  69.0 2.6 %collective-permute-start.27 = (bf16[256,128]{1,0:T(8,128)(2,1)S(1)}, bf16[256,128]{1,0:T(8,128)(2,1)S(1)}, u32[]{:S(2)}, u32[]{:S(2)}) collective-permute-start(bf16[256,128]{1,0:T(8,128)(2,1)S(1)} %get-tuple-element.47), channel_id=1, source_target_pairs={{0,64},{16,80},{32,96},{48,112},{64,128},{80,144},{96,160},{112,17... | collective-permute-start | bytes 196616 | tf_op jit(solution)/shard_map/ppermute | solution.py:22
  71.6 1.2 %collective-permute-start.26 = (bf16[256,128]{1,0:T(8,128)(2,1)S(1)}, bf16[256,128]{1,0:T(8,128)(2,1)S(1)}, u32[]{:S(2)}, u32[]{:S(2)}) collective-permute-start(bf16[256,128]{1,0:T(8,128)(2,1)S(1)} %get-tuple-element.48), channel_id=1, source_target_pairs={{0,192},{16,208},{32,224},{48,240},{64,0},{80,16},{96,32},{112,48}... | collective-permute-start | bytes 196616 | tf_op jit(solution)/shard_map/ppermute | solution.py:22
  73.0 1.5 %collective-permute-done.27 = bf16[256,128]{1,0:T(8,128)(2,1)S(1)} collective-permute-done((bf16[256,128]{1,0:T(8,128)(2,1)S(1)}, bf16[256,128]{1,0:T(8,128)(2,1)S(1)}, u32[]{:S(2)}, u32[]{:S(2)}) %collective-permute-start.27) | collective-permute-done | bytes 65568 | tf_op jit(solution)/shard_map/ppermute | solution.py:22
  74.5 1.4 %collective-permute-done.26 = bf16[256,128]{1,0:T(8,128)(2,1)S(1)} collective-permute-done((bf16[256,128]{1,0:T(8,128)(2,1)S(1)}, bf16[256,128]{1,0:T(8,128)(2,1)S(1)}, u32[]{:S(2)}, u32[]{:S(2)}) %collective-permute-start.26) | collective-permute-done | bytes 65568 | tf_op jit(solution)/shard_map/ppermute | solution.py:22
  77.4 4.4 %collective-permute-done.28 = bf16[2,2,64,128]{3,0,2,1:T(2,128)(2,1)S(1)} collective-permute-done((bf16[2,2,64,128]{3,0,2,1:T(2,128)(2,1)S(1)}, bf16[2,2,64,128]{3,0,2,1:T(2,128)(2,1)S(1)}, u32[]{:S(2)}, u32[]{:S(2)}) %collective-permute-start.28) | collective-permute-done | bytes 65568 | tf_op jit(solution)/shard_map/ppermute | solution.py:26
  (74 shorter events, 13.1 us)
Async XLA Ops:
  0.6 2.5 %copy-start = (bf16[256,2,2,128]{3,2,1,0:T(2,128)(2,1)S(1)}, bf16[256,2,2,128]{3,2,1,0:T(2,128)(2,1)}, u32[]{:S(2)}) copy-start(bf16[256,2,2,128]{3,2,1,0:T(2,128)(2,1)} %param.11) | copy-start | bytes 786436
  1.5 7.2 %collective-permute-start.2 = (bf16[2,2,64,128]{3,2,1,0:T(8,128)(2,1)S(1)}, bf16[2,2,64,128]{3,2,1,0:T(8,128)(2,1)S(1)}, u32[]{:S(2)}, u32[]{:S(2)}) collective-permute-start(bf16[2,2,64,128]{3,2,1,0:T(8,128)(2,1)S(1)} %maximum_bitcast_fusion.1), channel_id=1, source_target_pairs={{0,2},{1,3},{2,0},{3,1},{4,6},{5,7},{6,4},{7,5},{8,10},{9,11},{10,... | collective-permute-start | bytes 196616 | tf_op jit(solution)/shard_map/ppermute | solution.py:26
  4.9 2.1 %copy-start.3 = (s32[1,2,2,8]{3,2,1,0:T(2,128)S(1)}, s32[1,2,2,8]{3,2,1,0:T(2,128)}, u32[]{:S(2)}) copy-start(s32[1,2,2,8]{3,2,1,0:T(2,128)} %param.13) | copy-start | bytes 388
  4.9 2.1 %copy-start.1 = (bf16[256,2,2,128]{3,2,1,0:T(2,128)(2,1)S(1)}, bf16[256,2,2,128]{3,2,1,0:T(2,128)(2,1)}, u32[]{:S(2)}) copy-start(bf16[256,2,2,128]{3,2,1,0:T(2,128)(2,1)} %param.10) | copy-start | bytes 786436
  5.0 29.3 %collective-permute-start.1 = (bf16[2,4,256,128]{3,2,1,0:T(8,128)(2,1)S(1)}, bf16[2,4,256,128]{3,2,1,0:T(8,128)(2,1)S(1)}, u32[]{:S(2)}, u32[]{:S(2)}) collective-permute-start(bf16[2,4,256,128]{3,2,1,0:T(8,128)(2,1)S(1)} %bitcast.77), channel_id=1, source_target_pairs={{0,1},{1,0},{2,3},{3,2},{4,5},{5,4},{6,7},{7,6},{8,9},{9,8},{10,11... | collective-permute-start | bytes 1572872 | tf_op jit(solution)/shard_map/ppermute | solution.py:26
  8.8 7.5 %collective-permute-start.8 = (bf16[256,128]{1,0:T(8,128)(2,1)S(1)}, bf16[256,128]{1,0:T(8,128)(2,1)S(1)}, u32[]{:S(2)}, u32[]{:S(2)}) collective-permute-start(bf16[256,128]{1,0:T(8,128)(2,1)S(1)} %bitcast.90), channel_id=1, source_target_pairs={{0,192},{16,208},{32,224},{48,240},{64,0},{80,16},{96,32},{112,48}... | collective-permute-start | bytes 196616 | tf_op jit(solution)/shard_map/ppermute | solution.py:22
  11.9 5.8 %collective-permute-start.7 = (bf16[256,128]{1,0:T(8,128)(2,1)S(1)}, bf16[256,128]{1,0:T(8,128)(2,1)S(1)}, u32[]{:S(2)}, u32[]{:S(2)}) collective-permute-start(bf16[256,128]{1,0:T(8,128)(2,1)S(1)} %bitcast.91), channel_id=1, source_target_pairs={{0,128},{16,144},{32,160},{48,176},{64,192},{80,208},{96,224},{112... | collective-permute-start | bytes 196616 | tf_op jit(solution)/shard_map/ppermute | solution.py:22
  12.5 6.7 %collective-permute-start.6 = (bf16[256,128]{1,0:T(8,128)(2,1)S(1)}, bf16[256,128]{1,0:T(8,128)(2,1)S(1)}, u32[]{:S(2)}, u32[]{:S(2)}) collective-permute-start(bf16[256,128]{1,0:T(8,128)(2,1)S(1)} %bitcast.92), channel_id=1, source_target_pairs={{0,64},{16,80},{32,96},{48,112},{64,128},{80,144},{96,160},{112,17... | collective-permute-start | bytes 196616 | tf_op jit(solution)/shard_map/ppermute | solution.py:22
  13.5 7.3 %collective-permute-start.5 = (bf16[256,128]{1,0:T(8,128)(2,1)S(1)}, bf16[256,128]{1,0:T(8,128)(2,1)S(1)}, u32[]{:S(2)}, u32[]{:S(2)}) collective-permute-start(bf16[256,128]{1,0:T(8,128)(2,1)S(1)} %bitcast.86), channel_id=1, source_target_pairs={{0,48},{16,0},{32,16},{48,32},{64,112},{80,64},{96,80},{112,96},{1... | collective-permute-start | bytes 196616 | tf_op jit(solution)/shard_map/ppermute | solution.py:22
  16.2 6.5 %collective-permute-start.4 = (bf16[256,128]{1,0:T(8,128)(2,1)S(1)}, bf16[256,128]{1,0:T(8,128)(2,1)S(1)}, u32[]{:S(2)}, u32[]{:S(2)}) collective-permute-start(bf16[256,128]{1,0:T(8,128)(2,1)S(1)} %bitcast.87), channel_id=1, source_target_pairs={{0,32},{16,48},{32,0},{48,16},{64,96},{80,112},{96,64},{112,80},{1... | collective-permute-start | bytes 196616 | tf_op jit(solution)/shard_map/ppermute | solution.py:22
  17.7 6.3 %collective-permute-start.3 = (bf16[256,128]{1,0:T(8,128)(2,1)S(1)}, bf16[256,128]{1,0:T(8,128)(2,1)S(1)}, u32[]{:S(2)}, u32[]{:S(2)}) collective-permute-start(bf16[256,128]{1,0:T(8,128)(2,1)S(1)} %bitcast.88), channel_id=1, source_target_pairs={{0,16},{16,32},{32,48},{48,0},{64,80},{80,96},{96,112},{112,64},{1... | collective-permute-start | bytes 196616 | tf_op jit(solution)/shard_map/ppermute | solution.py:22
  19.2 12.0 %collective-permute-start.11 = (bf16[4,256,128]{2,1,0:T(8,128)(2,1)S(1)}, bf16[4,256,128]{2,1,0:T(8,128)(2,1)S(1)}, u32[]{:S(2)}, u32[]{:S(2)}) collective-permute-start(bf16[4,256,128]{2,1,0:T(8,128)(2,1)S(1)} %pad_maximum_fusion.1.refs_5_), channel_id=1, source_target_pairs={{0,16},{16,32},{32,48},{48,0},{64,80},{80,96},{96,112},{112,64},{1... | collective-permute-start | bytes 786440 | tf_op jit(solution)/shard_map/ppermute | solution.py:22
  24.0 8.8 %collective-permute-start.9 = (bf16[4,256,128]{2,1,0:T(8,128)(2,1)S(1)}, bf16[4,256,128]{2,1,0:T(8,128)(2,1)S(1)}, u32[]{:S(2)}, u32[]{:S(2)}) collective-permute-start(bf16[4,256,128]{2,1,0:T(8,128)(2,1)S(1)} %pad_maximum_fusion.refs_4_), channel_id=1, source_target_pairs={{0,64},{16,80},{32,96},{48,112},{64,128},{80,144},{96,160},{112,17... | collective-permute-start | bytes 786440 | tf_op jit(solution)/shard_map/ppermute | solution.py:22
  25.7 3.8 %collective-permute-start = (f32[3,4,256]{2,1,0:T(4,128)S(1)}, f32[3,4,256]{2,1,0:T(4,128)S(1)}, u32[]{:S(2)}, u32[]{:S(2)}) collective-permute-start(f32[3,4,256]{2,1,0:T(4,128)S(1)} %constant_dynamic-update-slice_fusion), channel_id=1, source_target_pairs={{0,1},{1,0},{2,3},{3,2},{4,5},{5,4},{6,7},{7,6},{8,9},{9,8},{10,11... | collective-permute-start | bytes 36872 | tf_op jit(solution)/shard_map/ppermute | solution.py:26
  26.5 9.7 %collective-permute-start.14 = (bf16[4,256,128]{2,1,0:T(8,128)(2,1)S(1)}, bf16[4,256,128]{2,1,0:T(8,128)(2,1)S(1)}, u32[]{:S(2)}, u32[]{:S(2)}) collective-permute-start(bf16[4,256,128]{2,1,0:T(8,128)(2,1)S(1)} %pad_maximum_fusion.1.refs_5_), channel_id=1, source_target_pairs={{0,48},{16,0},{32,16},{48,32},{64,112},{80,64},{96,80},{112,96},{1... | collective-permute-start | bytes 786440 | tf_op jit(solution)/shard_map/ppermute | solution.py:22
  29.5 6.8 %collective-permute-start.13 = (bf16[4,256,128]{2,1,0:T(8,128)(2,1)S(1)}, bf16[4,256,128]{2,1,0:T(8,128)(2,1)S(1)}, u32[]{:S(2)}, u32[]{:S(2)}) collective-permute-start(bf16[4,256,128]{2,1,0:T(8,128)(2,1)S(1)} %pad_maximum_fusion.refs_4_), channel_id=1, source_target_pairs={{0,192},{16,208},{32,224},{48,240},{64,0},{80,16},{96,32},{112,48}... | collective-permute-start | bytes 786440 | tf_op jit(solution)/shard_map/ppermute | solution.py:22
  31.2 7.6 %collective-permute-start.12 = (bf16[4,256,128]{2,1,0:T(8,128)(2,1)S(1)}, bf16[4,256,128]{2,1,0:T(8,128)(2,1)S(1)}, u32[]{:S(2)}, u32[]{:S(2)}) collective-permute-start(bf16[4,256,128]{2,1,0:T(8,128)(2,1)S(1)} %collective-permute-done.11.refs_6_), channel_id=1, source_target_pairs={{0,16},{16,32},{32,48},{48,0},{64,80},{80,96},{96,112},{112,64},{1... | collective-permute-start | bytes 786440 | tf_op jit(solution)/shard_map/ppermute | solution.py:22
  32.8 7.6 %collective-permute-start.10 = (bf16[4,256,128]{2,1,0:T(8,128)(2,1)S(1)}, bf16[4,256,128]{2,1,0:T(8,128)(2,1)S(1)}, u32[]{:S(2)}, u32[]{:S(2)}) collective-permute-start(bf16[4,256,128]{2,1,0:T(8,128)(2,1)S(1)} %collective-permute-done.9.refs_4_), channel_id=1, source_target_pairs={{0,64},{16,80},{32,96},{48,112},{64,128},{80,144},{96,160},{112,17... | collective-permute-start | bytes 786440 | tf_op jit(solution)/shard_map/ppermute | solution.py:22
  41.2 12.2 %collective-permute-start.16 = (bf16[4,256,128]{2,1,0:T(8,128)(2,1)S(1)}, bf16[4,256,128]{2,1,0:T(8,128)(2,1)S(1)}, u32[]{:S(2)}, u32[]{:S(2)}) collective-permute-start(bf16[4,256,128]{2,1,0:T(8,128)(2,1)S(1)} %get-tuple-element.27), channel_id=1, source_target_pairs={{0,192},{16,208},{32,224},{48,240},{64,0},{80,16},{96,32},{112,48}... | collective-permute-start | bytes 786440 | tf_op jit(solution)/shard_map/ppermute | solution.py:22
  47.9 13.1 %collective-permute-start.18 = (bf16[4,256,128]{2,1,0:T(8,128)(2,1)S(1)}, bf16[4,256,128]{2,1,0:T(8,128)(2,1)S(1)}, u32[]{:S(2)}, u32[]{:S(2)}) collective-permute-start(bf16[4,256,128]{2,1,0:T(8,128)(2,1)S(1)} %get-tuple-element.32), channel_id=1, source_target_pairs={{0,64},{16,80},{32,96},{48,112},{64,128},{80,144},{96,160},{112,17... | collective-permute-start | bytes 786440 | tf_op jit(solution)/shard_map/ppermute | solution.py:22
  47.9 9.9 %collective-permute-start.22 = (bf16[4,256,128]{2,1,0:T(8,128)(2,1)S(1)}, bf16[4,256,128]{2,1,0:T(8,128)(2,1)S(1)}, u32[]{:S(2)}, u32[]{:S(2)}) collective-permute-start(bf16[4,256,128]{2,1,0:T(8,128)(2,1)S(1)} %get-tuple-element.33), channel_id=1, source_target_pairs={{0,48},{16,0},{32,16},{48,32},{64,112},{80,64},{96,80},{112,96},{1... | collective-permute-start | bytes 786440 | tf_op jit(solution)/shard_map/ppermute | solution.py:22
  53.5 7.7 %collective-permute-start.17 = (bf16[4,256,128]{2,1,0:T(8,128)(2,1)S(1)}, bf16[4,256,128]{2,1,0:T(8,128)(2,1)S(1)}, u32[]{:S(2)}, u32[]{:S(2)}) collective-permute-start(bf16[4,256,128]{2,1,0:T(8,128)(2,1)S(1)} %add_convert_fusion.1), channel_id=1, source_target_pairs={{0,192},{16,208},{32,224},{48,240},{64,0},{80,16},{96,32},{112,48}... | collective-permute-start | bytes 786440 | tf_op jit(solution)/shard_map/ppermute | solution.py:22
  57.2 8.3 %collective-permute-start.24 = (bf16[4,256,128]{2,1,0:T(8,128)(2,1)S(1)}, bf16[4,256,128]{2,1,0:T(8,128)(2,1)S(1)}, u32[]{:S(2)}, u32[]{:S(2)}) collective-permute-start(bf16[4,256,128]{2,1,0:T(8,128)(2,1)S(1)} %get-tuple-element.38), channel_id=1, source_target_pairs={{0,16},{16,32},{32,48},{48,0},{64,80},{80,96},{96,112},{112,64},{1... | collective-permute-start | bytes 786440 | tf_op jit(solution)/shard_map/ppermute | solution.py:22
  57.4 19.0 %collective-permute-start.15 = (bf16[4,256,128]{2,1,0:T(8,128)(2,1)S(1)}, bf16[4,256,128]{2,1,0:T(8,128)(2,1)S(1)}, u32[]{:S(2)}, u32[]{:S(2)}) collective-permute-start(bf16[4,256,128]{2,1,0:T(8,128)(2,1)S(1)} %get-tuple-element.26), channel_id=1, source_target_pairs={{0,1},{1,0},{2,3},{3,2},{4,5},{5,4},{6,7},{7,6},{8,9},{9,8},{10,11... | collective-permute-start | bytes 786440 | tf_op jit(solution)/shard_map/ppermute | solution.py:26
  57.9 9.0 %collective-permute-start.23 = (bf16[4,256,128]{2,1,0:T(8,128)(2,1)S(1)}, bf16[4,256,128]{2,1,0:T(8,128)(2,1)S(1)}, u32[]{:S(2)}, u32[]{:S(2)}) collective-permute-start(bf16[4,256,128]{2,1,0:T(8,128)(2,1)S(1)} %add_convert_fusion), channel_id=1, source_target_pairs={{0,48},{16,0},{32,16},{48,32},{64,112},{80,64},{96,80},{112,96},{1... | collective-permute-start | bytes 786440 | tf_op jit(solution)/shard_map/ppermute | solution.py:22
  61.2 7.8 %collective-permute-start.19 = (bf16[256,128]{1,0:T(8,128)(2,1)S(1)}, bf16[256,128]{1,0:T(8,128)(2,1)S(1)}, u32[]{:S(2)}, u32[]{:S(2)}) collective-permute-start(bf16[256,128]{1,0:T(8,128)(2,1)S(1)} %get-tuple-element.43), channel_id=1, source_target_pairs={{0,32},{16,48},{32,0},{48,16},{64,96},{80,112},{96,64},{112,80},{1... | collective-permute-start | bytes 196616 | tf_op jit(solution)/shard_map/ppermute | solution.py:22
  63.6 8.0 %collective-permute-start.21 = (bf16[256,128]{1,0:T(8,128)(2,1)S(1)}, bf16[256,128]{1,0:T(8,128)(2,1)S(1)}, u32[]{:S(2)}, u32[]{:S(2)}) collective-permute-start(bf16[256,128]{1,0:T(8,128)(2,1)S(1)} %get-tuple-element.44), channel_id=1, source_target_pairs={{0,16},{16,32},{32,48},{48,0},{64,80},{80,96},{96,112},{112,64},{1... | collective-permute-start | bytes 196616 | tf_op jit(solution)/shard_map/ppermute | solution.py:22
  65.5 7.2 %collective-permute-start.20 = (bf16[256,128]{1,0:T(8,128)(2,1)S(1)}, bf16[256,128]{1,0:T(8,128)(2,1)S(1)}, u32[]{:S(2)}, u32[]{:S(2)}) collective-permute-start(bf16[256,128]{1,0:T(8,128)(2,1)S(1)} %get-tuple-element.45), channel_id=1, source_target_pairs={{0,48},{16,0},{32,16},{48,32},{64,112},{80,64},{96,80},{112,96},{1... | collective-permute-start | bytes 196616 | tf_op jit(solution)/shard_map/ppermute | solution.py:22
  67.0 6.0 %collective-permute-start.25 = (bf16[256,128]{1,0:T(8,128)(2,1)S(1)}, bf16[256,128]{1,0:T(8,128)(2,1)S(1)}, u32[]{:S(2)}, u32[]{:S(2)}) collective-permute-start(bf16[256,128]{1,0:T(8,128)(2,1)S(1)} %get-tuple-element.46), channel_id=1, source_target_pairs={{0,128},{16,144},{32,160},{48,176},{64,192},{80,208},{96,224},{112... | collective-permute-start | bytes 196616 | tf_op jit(solution)/shard_map/ppermute | solution.py:22
  69.0 5.5 %collective-permute-start.27 = (bf16[256,128]{1,0:T(8,128)(2,1)S(1)}, bf16[256,128]{1,0:T(8,128)(2,1)S(1)}, u32[]{:S(2)}, u32[]{:S(2)}) collective-permute-start(bf16[256,128]{1,0:T(8,128)(2,1)S(1)} %get-tuple-element.47), channel_id=1, source_target_pairs={{0,64},{16,80},{32,96},{48,112},{64,128},{80,144},{96,160},{112,17... | collective-permute-start | bytes 196616 | tf_op jit(solution)/shard_map/ppermute | solution.py:22
  71.6 4.3 %collective-permute-start.26 = (bf16[256,128]{1,0:T(8,128)(2,1)S(1)}, bf16[256,128]{1,0:T(8,128)(2,1)S(1)}, u32[]{:S(2)}, u32[]{:S(2)}) collective-permute-start(bf16[256,128]{1,0:T(8,128)(2,1)S(1)} %get-tuple-element.48), channel_id=1, source_target_pairs={{0,192},{16,208},{32,224},{48,240},{64,0},{80,16},{96,32},{112,48}... | collective-permute-start | bytes 196616 | tf_op jit(solution)/shard_map/ppermute | solution.py:22
  76.3 5.6 %collective-permute-start.28 = (bf16[2,2,64,128]{3,0,2,1:T(2,128)(2,1)S(1)}, bf16[2,2,64,128]{3,0,2,1:T(2,128)(2,1)S(1)}, u32[]{:S(2)}, u32[]{:S(2)}) collective-permute-start(bf16[2,2,64,128]{3,0,2,1:T(2,128)(2,1)S(1)} %fusion.8), channel_id=1, source_target_pairs={{0,2},{1,3},{2,0},{3,1},{4,6},{5,7},{6,4},{7,5},{8,10},{9,11},{10,... | collective-permute-start | bytes 196616 | tf_op jit(solution)/shard_map/ppermute | solution.py:26
  (1 other events, 0.7 us)
where the time goes:
time: 84 us; the launch traced here: 82.8 us
  starting transfers between devices  48.9 us (58%)
  waiting for transfers between devices  18.5 us (22%)
  Pallas kernels  7 us (8%)
  local copies, waits for them, and re-layouts  3.73 us (4%)
  other arithmetic  3.7 us (4%)
  between operations  0.9 us (1%)
    ppermute x24, starting transfers between devices, move(): return lax.ppermute(array, 'ctx', shifts(rows, columns))  43.8 us
    ppermute x24, waiting for transfers between devices, move(): return lax.ppermute(array, 'ctx', shifts(rows, columns))  12.2 us
    ppermute x5, waiting for transfers between devices, swap(): return lax.ppermute(array, 'dp', [(d, d ^ bit) for d in range(4)])  6.35 us
    ppermute x5, starting transfers between devices, swap(): return lax.ppermute(array, 'dp', [(d, d ^ bit) for d in range(4)])  5.04 us
    pallas_call x3, Pallas kernels, attend_call(): pl.pallas_call(lambda *refs: attend(*refs, which=which, parts=parts, scal...  4.99 us
    pallas_call x1, Pallas kernels, plan_call(): pl.pallas_call(lambda *refs: plan(*refs, pairs=pairs), out_shape=[jax.Sha...  2.02 us
    transpose x1, other arithmetic, step(): jnp.stack([queries, grad_out]).transpose(0, 2, 3, 1, 4)  1.73 us
  transfers between devices with their start and end apart: 29, of which 12 were waited for; matrix products, arithmetic and copies ran while one was open for 6% of the time, Pallas kernels for 7%

commit v1 on v0

--- a/solution.py
+++ b/solution.py
@@ -10,16 +10,23 @@
 SIDE = 4
 
 
-def shifts(rows, columns):
-    return [
+def move(array, rows, columns, kept=range(SIDE)):
+    pairs = [
         (y * SIDE + x, (y + rows) % SIDE * SIDE + (x + columns) % SIDE)
-        for y in range(SIDE)
+        for y in kept
         for x in range(SIDE)
     ]
-
-
-def move(array, rows, columns):
-    return lax.ppermute(array, "ctx", shifts(rows, columns))
+    return lax.ppermute(array, "ctx", pairs)
+
+
+def senders(rows, distance, lead=0):
+    every = range(SIDE)
+    return [y for y in every if 0 <= y - lead < SIDE - distance] if rows else every
+
+
+def returners(rows, distance):
+    every = range(SIDE)
+    return [y for y in every if y >= distance] if rows else every
 
 
 def swap(array, bit):
@@ -27,32 +34,34 @@
 
 
 def gather_small(own, rows, columns):
-    before = move(own, rows, columns)
-    after = move(own, -rows, -columns)
-    far = move(own, 2 * rows, 2 * columns)
+    before = move(own, rows, columns, senders(rows, 1))
+    after = move(own, -rows, -columns, senders(rows, 3))
+    far = move(own, 2 * rows, 2 * columns, senders(rows, 2))
     return jnp.stack([own, before, far, after])
 
 
 def gather_large(own, rows, columns):
-    before = move(own, rows, columns)
-    after = move(own, -rows, -columns)
-    far = move(before, rows, columns)
+    before = move(own, rows, columns, senders(rows, 1))
+    after = move(own, -rows, -columns, senders(rows, 3))
+    far = move(before, rows, columns, senders(rows, 2, 1))
     return own, before, after, far
 
 
 def reduce_large(own, before, after, far, rows, columns):
     full = jnp.float32
-    after = move(after, rows, columns)
-    far, own = lax.optimization_barrier((move(far, -rows, -columns), own))
-    before = move((before.astype(full) + far.astype(full)).astype(before.dtype), -rows, -columns)
+    after = move(after, rows, columns, returners(rows, 3))
+    far = move(far, -rows, -columns, returners(rows, 2))
+    far, own = lax.optimization_barrier((far, own))
+    near = (before.astype(full) + far.astype(full)).astype(before.dtype)
+    before = move(near, -rows, -columns, returners(rows, 1))
     return own + before.astype(full) + after.astype(full)
 
 
 def reduce_small(terms, rows, columns):
     full, low = jnp.float32, terms.astype(jnp.bfloat16)
-    far = move(low[2], -2 * rows, -2 * columns)
-    before = move(low[1], -rows, -columns)
-    after = move(low[3], rows, columns)
+    far = move(low[2], -2 * rows, -2 * columns, returners(rows, 2))
+    before = move(low[1], -rows, -columns, returners(rows, 1))
+    after = move(low[3], rows, columns, returners(rows, 3))
     return terms[0] + far.astype(full) + before.astype(full) + after.astype(full)
 
 
@@ -296,7 +305,8 @@
     own_0, before_0, after_0, far_0 = gather_large(gather_small(kv[0], 0, 1), 1, 0)
     own_1, before_1, after_1, far_1 = gather_large(gather_small(kv[1], 1, 0), 0, 1)
 
-    delta = jnp.sum(grad_out.astype(full) * forward_out.astype(full), axis=-1).transpose(1, 2, 0)
+    delta = jnp.sum(grad_out.astype(full) * forward_out.astype(full), axis=-1)
+    delta = delta.transpose(1, 2, 0)
     ids = jnp.pad(selected[0].astype(full), ((0, 0), (0, 0), (0, BLOCK - selected.shape[-1])))
     small = jnp.stack([logsumexp, delta, ids]).reshape(3, pairs, BLOCK)
     small_far = swap(small, 1)

time: 84 us -> 89.7 us (1.068)
  waiting for transfers between devices: 18.5 us -> 30.1 us
  starting transfers between devices: 48.9 us -> 42.4 us
    ppermute x24, waiting for transfers between devices: 12.2 us -> 23.4 us  [move(): return lax.ppermute(array, 'ctx', pairs)]
    ppermute x24, starting transfers between devices: 43.8 us -> 36.7 us  [move(): return lax.ppermute(array, 'ctx', pairs)]
where the time goes in v1:
time: 89.7 us; the launch traced here: 88 us
  starting transfers between devices  42.4 us (47%)
  waiting for transfers between devices  30.1 us (34%)
  Pallas kernels  7 us (8%)
  local copies, waits for them, and re-layouts  3.73 us (4%)
  other arithmetic  3.71 us (4%)
  between operations  1.03 us (1%)
    ppermute x24, starting transfers between devices, move(): return lax.ppermute(array, 'ctx', pairs)  36.7 us
    ppermute x24, waiting for transfers between devices, move(): return lax.ppermute(array, 'ctx', pairs)  23.4 us
    ppermute x5, waiting for transfers between devices, swap(): return lax.ppermute(array, 'dp', [(d, d ^ bit) for d in range(4)])  6.72 us
    ppermute x5, starting transfers between devices, swap(): return lax.ppermute(array, 'dp', [(d, d ^ bit) for d in range(4)])  5.68 us
    pallas_call x3, Pallas kernels, attend_call(): pl.pallas_call(lambda *refs: attend(*refs, which=which, parts=parts, scal...  4.98 us
    pallas_call x1, Pallas kernels, plan_call(): pl.pallas_call(lambda *refs: plan(*refs, pairs=pairs), out_shape=[jax.Sha...  2.02 us
  transfers between devices with their start and end apart: 29, of which 12 were waited for; matrix products, arithmetic and copies ran while one was open for 6% of the time, Pallas kernels for 7%

profile of v1, /device:TPU:0, one launch (start us, length us, event | category | flops | bytes accessed | tf_op | source)
XLA Modules:
  0.0 88.0 jit_solution(4550518534252737096)
XLA Ops:
  1.5 1.6 %collective-permute-start.2 = (bf16[2,2,64,128]{3,2,1,0:T(8,128)(2,1)S(1)}, bf16[2,2,64,128]{3,2,1,0:T(8,128)(2,1)S(1)}, u32[]{:S(2)}, u32[]{:S(2)}) collective-permute-start(bf16[2,2,64,128]{3,2,1,0:T(8,128)(2,1)S(1)} %maximum_bitcast_fusion.1), channel_id=1, source_target_pairs={{0,2},{1,3},{2,0},{3,1},{4,6},{5,7},{6,4},{7,5},{8,10},{9,11},{10,... | collective-permute-start | bytes 196616 | tf_op jit(solution)/shard_map/ppermute | solution.py:33
  3.1 1.7 %maximum_bitcast_fusion = bf16[2,2,2,256,128]{4,2,1,3,0:T(2,128)(2,1)S(1)} fusion(bf16[1,256,2,2,128]{4,3,2,1,0:T(2,128)(2,1)S(1)} %bitcast.80, bf16[1,256,2,2,128]{4,3,2,1,0:T(2,128)(2,1)} %bitcast.85), kind=kLoop, calls=%fused_computation | loop fusion | flops 262144 | bytes 1048576 | tf_op jit(solution)/shard_map/transpose | solution.py:302
  5.0 2.0 %collective-permute-start.1 = (bf16[2,4,256,128]{3,2,1,0:T(8,128)(2,1)S(1)}, bf16[2,4,256,128]{3,2,1,0:T(8,128)(2,1)S(1)}, u32[]{:S(2)}, u32[]{:S(2)}) collective-permute-start(bf16[2,4,256,128]{3,2,1,0:T(8,128)(2,1)S(1)} %bitcast.77), channel_id=1, source_target_pairs={{0,1},{1,0},{2,3},{3,2},{4,5},{5,4},{6,7},{7,6},{8,9},{9,8},{10,11... | collective-permute-start | bytes 1572872 | tf_op jit(solution)/shard_map/ppermute | solution.py:33
  8.8 4.9 %collective-permute-start.8 = (bf16[256,128]{1,0:T(8,128)(2,1)S(1)}, bf16[256,128]{1,0:T(8,128)(2,1)S(1)}, u32[]{:S(2)}, u32[]{:S(2)}) collective-permute-start(bf16[256,128]{1,0:T(8,128)(2,1)S(1)} %bitcast.90), channel_id=1, source_target_pairs={{0,192},{16,208},{32,224},{48,240},{1,193},{17,209},{33,225},{49,2... | collective-permute-start | bytes 196616 | tf_op jit(solution)/shard_map/ppermute | solution.py:19
  13.7 1.3 %collective-permute-start.7 = (bf16[256,128]{1,0:T(8,128)(2,1)S(1)}, bf16[256,128]{1,0:T(8,128)(2,1)S(1)}, u32[]{:S(2)}, u32[]{:S(2)}) collective-permute-start(bf16[256,128]{1,0:T(8,128)(2,1)S(1)} %bitcast.91), channel_id=1, source_target_pairs={{0,128},{16,144},{32,160},{48,176},{64,192},{80,208},{96,224},{112... | collective-permute-start | bytes 196616 | tf_op jit(solution)/shard_map/ppermute | solution.py:19
  15.0 2.8 %collective-permute-start.6 = (bf16[256,128]{1,0:T(8,128)(2,1)S(1)}, bf16[256,128]{1,0:T(8,128)(2,1)S(1)}, u32[]{:S(2)}, u32[]{:S(2)}) collective-permute-start(bf16[256,128]{1,0:T(8,128)(2,1)S(1)} %bitcast.92), channel_id=1, source_target_pairs={{0,64},{16,80},{32,96},{48,112},{64,128},{80,144},{96,160},{112,17... | collective-permute-start | bytes 196616 | tf_op jit(solution)/shard_map/ppermute | solution.py:19
  17.8 2.8 %collective-permute-start.5 = (bf16[256,128]{1,0:T(8,128)(2,1)S(1)}, bf16[256,128]{1,0:T(8,128)(2,1)S(1)}, u32[]{:S(2)}, u32[]{:S(2)}) collective-permute-start(bf16[256,128]{1,0:T(8,128)(2,1)S(1)} %bitcast.86), channel_id=1, source_target_pairs={{0,48},{16,0},{32,16},{48,32},{64,112},{80,64},{96,80},{112,96},{1... | collective-permute-start | bytes 196616 | tf_op jit(solution)/shard_map/ppermute | solution.py:19
  22.4 1.9 %collective-permute-start.11 = (bf16[4,256,128]{2,1,0:T(8,128)(2,1)S(1)}, bf16[4,256,128]{2,1,0:T(8,128)(2,1)S(1)}, u32[]{:S(2)}, u32[]{:S(2)}) collective-permute-start(bf16[4,256,128]{2,1,0:T(8,128)(2,1)S(1)} %pad_maximum_fusion.1.refs_5_), channel_id=1, source_target_pairs={{0,16},{16,32},{32,48},{48,0},{64,80},{80,96},{96,112},{112,64},{1... | collective-permute-start | bytes 786440 | tf_op jit(solution)/shard_map/ppermute | solution.py:19
  24.2 2.9 %collective-permute-done.4 = bf16[256,128]{1,0:T(8,128)(2,1)S(1)} collective-permute-done((bf16[256,128]{1,0:T(8,128)(2,1)S(1)}, bf16[256,128]{1,0:T(8,128)(2,1)S(1)}, u32[]{:S(2)}, u32[]{:S(2)}) %collective-permute-start.4) | collective-permute-done | bytes 65568 | tf_op jit(solution)/shard_map/ppermute | solution.py:19
  28.1 1.9 %collective-permute-start.9 = (bf16[4,256,128]{2,1,0:T(8,128)(2,1)S(1)}, bf16[4,256,128]{2,1,0:T(8,128)(2,1)S(1)}, u32[]{:S(2)}, u32[]{:S(2)}) collective-permute-start(bf16[4,256,128]{2,1,0:T(8,128)(2,1)S(1)} %pad_maximum_fusion.refs_4_), channel_id=1, source_target_pairs={{0,64},{16,80},{32,96},{48,112},{64,128},{80,144},{96,160},{112,17... | collective-permute-start | bytes 786440 | tf_op jit(solution)/shard_map/ppermute | solution.py:19
  30.9 1.0 %collective-permute-start.14 = (bf16[4,256,128]{2,1,0:T(8,128)(2,1)S(1)}, bf16[4,256,128]{2,1,0:T(8,128)(2,1)S(1)}, u32[]{:S(2)}, u32[]{:S(2)}) collective-permute-start(bf16[4,256,128]{2,1,0:T(8,128)(2,1)S(1)} %pad_maximum_fusion.1.refs_5_), channel_id=1, source_target_pairs={{0,48},{16,0},{32,16},{48,32},{64,112},{80,64},{96,80},{112,96},{1... | collective-permute-start | bytes 786440 | tf_op jit(solution)/shard_map/ppermute | solution.py:19
  31.9 1.9 %collective-permute-done = f32[3,4,256]{2,1,0:T(4,128)S(1)} collective-permute-done((f32[3,4,256]{2,1,0:T(4,128)S(1)}, f32[3,4,256]{2,1,0:T(4,128)S(1)}, u32[]{:S(2)}, u32[]{:S(2)}) %collective-permute-start) | collective-permute-done | bytes 12320 | tf_op jit(solution)/shard_map/ppermute | solution.py:33
  33.9 2.0 %collective-permute-start.13 = (bf16[4,256,128]{2,1,0:T(8,128)(2,1)S(1)}, bf16[4,256,128]{2,1,0:T(8,128)(2,1)S(1)}, u32[]{:S(2)}, u32[]{:S(2)}) collective-permute-start(bf16[4,256,128]{2,1,0:T(8,128)(2,1)S(1)} %pad_maximum_fusion.refs_4_), channel_id=1, source_target_pairs={{0,192},{16,208},{32,224},{48,240},{1,193},{17,209},{33,225},{49,2... | collective-permute-start | bytes 786440 | tf_op jit(solution)/shard_map/ppermute | solution.py:19
  36.7 2.0 %plan.1 = (s32[720]{0:T(1024)S(1)}, bf16[2,8,256,128]{3,2,1,0:T(8,128)(2,1)S(1)}) custom-call(s32[8,8]{1,0:T(8,128)S(1)} %fusion.10.refs_0_, s32[3]{0:T(128)S(1)} %pad_add_fusion.refs_1_, bf16[2,4,256,128]{3,2,1,0:T(8,128)(2,1)S(1)} %bitcast.78, bf16[2,4,256,128]{3,2,1,0:T(8,128)(2,1)S(1)} %collective-permute-done.1.refs_3_), custom_call_target="tpu_custom_call" | custom-call | flops 1048576 | bytes 4194304 | tf_op jit(solution)/shard_map/plan/pallas_call | solution.py:116
  40.7 2.9 %collective-permute-done.12.refs_5_ = bf16[4,256,128]{2,1,0:T(8,128)(2,1)S(1)} collective-permute-done((bf16[4,256,128]{2,1,0:T(8,128)(2,1)S(1)}, bf16[4,256,128]{2,1,0:T(8,128)(2,1)S(1)}, u32[]{:S(2)}, u32[]{:S(2)}) %collective-permute-start.12) | collective-permute-done | bytes 262176 | tf_op jit(solution)/shard_map/ppermute | solution.py:19
  45.2 1.3 %collective-permute-start.18 = (bf16[4,256,128]{2,1,0:T(8,128)(2,1)S(1)}, bf16[4,256,128]{2,1,0:T(8,128)(2,1)S(1)}, u32[]{:S(2)}, u32[]{:S(2)}) collective-permute-start(bf16[4,256,128]{2,1,0:T(8,128)(2,1)S(1)} %get-tuple-element.32), channel_id=1, source_target_pairs={{192,0},{208,16},{224,32},{240,48},{193,1},{209,17},{225,33},{241,... | collective-permute-start | bytes 786440 | tf_op jit(solution)/shard_map/ppermute | solution.py:19
  46.5 1.4 %collective-permute-start.22 = (bf16[4,256,128]{2,1,0:T(8,128)(2,1)S(1)}, bf16[4,256,128]{2,1,0:T(8,128)(2,1)S(1)}, u32[]{:S(2)}, u32[]{:S(2)}) collective-permute-start(bf16[4,256,128]{2,1,0:T(8,128)(2,1)S(1)} %get-tuple-element.33), channel_id=1, source_target_pairs={{0,48},{16,0},{32,16},{48,32},{64,112},{80,64},{96,80},{112,96},{1... | collective-permute-start | bytes 786440 | tf_op jit(solution)/shard_map/ppermute | solution.py:19
  47.9 3.2 %shard_map.96 = (f32[4,256,128]{2,1,0:T(8,128)S(1)}, f32[4,256,128]{2,1,0:T(8,128)S(1)}, f32[4,256,128]{2,1,0:T(8,128)S(1)}, bf16[4,256,128]{2,1,0:T(8,128)(2,1)S(1)}) custom-call(s32[720]{0:T(1024)S(1)} %get-tuple-element.21.refs_0_, s32[3]{0:T(128)S(1)} %pad_add_fusion.refs_1_, f32[16,256]{1,0:T(8,128)S(1)} %fusion.9.refs_2_, ...), custom_call_target="tpu_custom_call" | custom-call | flops 671088640 | bytes 6291456 | tf_op jit(solution)/shard_map/pallas_call | solution.py:266
  51.2 1.3 %collective-permute-start.17 = (bf16[4,256,128]{2,1,0:T(8,128)(2,1)S(1)}, bf16[4,256,128]{2,1,0:T(8,128)(2,1)S(1)}, u32[]{:S(2)}, u32[]{:S(2)}) collective-permute-start(bf16[4,256,128]{2,1,0:T(8,128)(2,1)S(1)} %add_convert_fusion.1), channel_id=1, source_target_pairs={{64,0},{80,16},{96,32},{112,48},{128,64},{144,80},{160,96},{176,11... | collective-permute-start | bytes 786440 | tf_op jit(solution)/shard_map/ppermute | solution.py:19
  53.3 1.0 %collective-permute-start.15 = (bf16[4,256,128]{2,1,0:T(8,128)(2,1)S(1)}, bf16[4,256,128]{2,1,0:T(8,128)(2,1)S(1)}, u32[]{:S(2)}, u32[]{:S(2)}) collective-permute-start(bf16[4,256,128]{2,1,0:T(8,128)(2,1)S(1)} %get-tuple-element.26), channel_id=1, source_target_pairs={{0,1},{1,0},{2,3},{3,2},{4,5},{5,4},{6,7},{7,6},{8,9},{9,8},{10,11... | collective-permute-start | bytes 786440 | tf_op jit(solution)/shard_map/ppermute | solution.py:33
  55.1 2.0 %collective-permute-start.23 = (bf16[4,256,128]{2,1,0:T(8,128)(2,1)S(1)}, bf16[4,256,128]{2,1,0:T(8,128)(2,1)S(1)}, u32[]{:S(2)}, u32[]{:S(2)}) collective-permute-start(bf16[4,256,128]{2,1,0:T(8,128)(2,1)S(1)} %add_convert_fusion), channel_id=1, source_target_pairs={{0,48},{16,0},{32,16},{48,32},{64,112},{80,64},{96,80},{112,96},{1... | collective-permute-start | bytes 786440 | tf_op jit(solution)/shard_map/ppermute | solution.py:19
  57.0 2.8 %collective-permute-done.18 = bf16[4,256,128]{2,1,0:T(8,128)(2,1)S(1)} collective-permute-done((bf16[4,256,128]{2,1,0:T(8,128)(2,1)S(1)}, bf16[4,256,128]{2,1,0:T(8,128)(2,1)S(1)}, u32[]{:S(2)}, u32[]{:S(2)}) %collective-permute-start.18) | collective-permute-done | bytes 262176 | tf_op jit(solution)/shard_map/ppermute | solution.py:19
  59.9 5.9 %collective-permute-done.17 = bf16[4,256,128]{2,1,0:T(8,128)(2,1)S(1)} collective-permute-done((bf16[4,256,128]{2,1,0:T(8,128)(2,1)S(1)}, bf16[4,256,128]{2,1,0:T(8,128)(2,1)S(1)}, u32[]{:S(2)}, u32[]{:S(2)}) %collective-permute-start.17) | collective-permute-done | bytes 262176 | tf_op jit(solution)/shard_map/ppermute | solution.py:19
  65.9 1.0 %collective-permute-start.19 = (bf16[256,128]{1,0:T(8,128)(2,1)S(1)}, bf16[256,128]{1,0:T(8,128)(2,1)S(1)}, u32[]{:S(2)}, u32[]{:S(2)}) collective-permute-start(bf16[256,128]{1,0:T(8,128)(2,1)S(1)} %get-tuple-element.43), channel_id=1, source_target_pairs={{0,32},{16,48},{32,0},{48,16},{64,96},{80,112},{96,64},{112,80},{1... | collective-permute-start | bytes 196616 | tf_op jit(solution)/shard_map/ppermute | solution.py:19
  67.0 2.2 %collective-permute-start.21 = (bf16[256,128]{1,0:T(8,128)(2,1)S(1)}, bf16[256,128]{1,0:T(8,128)(2,1)S(1)}, u32[]{:S(2)}, u32[]{:S(2)}) collective-permute-start(bf16[256,128]{1,0:T(8,128)(2,1)S(1)} %get-tuple-element.44), channel_id=1, source_target_pairs={{0,16},{16,32},{32,48},{48,0},{64,80},{80,96},{96,112},{112,64},{1... | collective-permute-start | bytes 196616 | tf_op jit(solution)/shard_map/ppermute | solution.py:19
  69.1 1.0 %collective-permute-start.20 = (bf16[256,128]{1,0:T(8,128)(2,1)S(1)}, bf16[256,128]{1,0:T(8,128)(2,1)S(1)}, u32[]{:S(2)}, u32[]{:S(2)}) collective-permute-start(bf16[256,128]{1,0:T(8,128)(2,1)S(1)} %get-tuple-element.45), channel_id=1, source_target_pairs={{0,48},{16,0},{32,16},{48,32},{64,112},{80,64},{96,80},{112,96},{1... | collective-permute-start | bytes 196616 | tf_op jit(solution)/shard_map/ppermute | solution.py:19
  70.3 1.3 %collective-permute-start.25 = (bf16[256,128]{1,0:T(8,128)(2,1)S(1)}, bf16[256,128]{1,0:T(8,128)(2,1)S(1)}, u32[]{:S(2)}, u32[]{:S(2)}) collective-permute-start(bf16[256,128]{1,0:T(8,128)(2,1)S(1)} %get-tuple-element.46), channel_id=1, source_target_pairs={{128,0},{144,16},{160,32},{176,48},{192,64},{208,80},{224,96},{240... | collective-permute-start | bytes 196616 | tf_op jit(solution)/shard_map/ppermute | solution.py:19
  71.8 1.3 %collective-permute-start.27 = (bf16[256,128]{1,0:T(8,128)(2,1)S(1)}, bf16[256,128]{1,0:T(8,128)(2,1)S(1)}, u32[]{:S(2)}, u32[]{:S(2)}) collective-permute-start(bf16[256,128]{1,0:T(8,128)(2,1)S(1)} %get-tuple-element.47), channel_id=1, source_target_pairs={{192,0},{208,16},{224,32},{240,48},{193,1},{209,17},{225,33},{241,... | collective-permute-start | bytes 196616 | tf_op jit(solution)/shard_map/ppermute | solution.py:19
  73.1 1.3 %collective-permute-start.26 = (bf16[256,128]{1,0:T(8,128)(2,1)S(1)}, bf16[256,128]{1,0:T(8,128)(2,1)S(1)}, u32[]{:S(2)}, u32[]{:S(2)}) collective-permute-start(bf16[256,128]{1,0:T(8,128)(2,1)S(1)} %get-tuple-element.48), channel_id=1, source_target_pairs={{64,0},{80,16},{96,32},{112,48},{128,64},{144,80},{160,96},{176,11... | collective-permute-start | bytes 196616 | tf_op jit(solution)/shard_map/ppermute | solution.py:19
  74.6 3.6 %collective-permute-done.25 = bf16[256,128]{1,0:T(8,128)(2,1)S(1)} collective-permute-done((bf16[256,128]{1,0:T(8,128)(2,1)S(1)}, bf16[256,128]{1,0:T(8,128)(2,1)S(1)}, u32[]{:S(2)}, u32[]{:S(2)}) %collective-permute-start.25) | collective-permute-done | bytes 65568 | tf_op jit(solution)/shard_map/ppermute | solution.py:19
  78.2 2.5 %collective-permute-done.27 = bf16[256,128]{1,0:T(8,128)(2,1)S(1)} collective-permute-done((bf16[256,128]{1,0:T(8,128)(2,1)S(1)}, bf16[256,128]{1,0:T(8,128)(2,1)S(1)}, u32[]{:S(2)}, u32[]{:S(2)}) %collective-permute-start.27) | collective-permute-done | bytes 65568 | tf_op jit(solution)/shard_map/ppermute | solution.py:19
  82.3 4.8 %collective-permute-done.28 = bf16[2,2,64,128]{3,0,2,1:T(2,128)(2,1)S(1)} collective-permute-done((bf16[2,2,64,128]{3,0,2,1:T(2,128)(2,1)S(1)}, bf16[2,2,64,128]{3,0,2,1:T(2,128)(2,1)S(1)}, u32[]{:S(2)}, u32[]{:S(2)}) %collective-permute-start.28) | collective-permute-done | bytes 65568 | tf_op jit(solution)/shard_map/ppermute | solution.py:33
  (74 shorter events, 15.3 us)
Async XLA Ops:
  0.6 2.5 %copy-start = (bf16[256,2,2,128]{3,2,1,0:T(2,128)(2,1)S(1)}, bf16[256,2,2,128]{3,2,1,0:T(2,128)(2,1)}, u32[]{:S(2)}) copy-start(bf16[256,2,2,128]{3,2,1,0:T(2,128)(2,1)} %param.11) | copy-start | bytes 786436
  1.5 7.2 %collective-permute-start.2 = (bf16[2,2,64,128]{3,2,1,0:T(8,128)(2,1)S(1)}, bf16[2,2,64,128]{3,2,1,0:T(8,128)(2,1)S(1)}, u32[]{:S(2)}, u32[]{:S(2)}) collective-permute-start(bf16[2,2,64,128]{3,2,1,0:T(8,128)(2,1)S(1)} %maximum_bitcast_fusion.1), channel_id=1, source_target_pairs={{0,2},{1,3},{2,0},{3,1},{4,6},{5,7},{6,4},{7,5},{8,10},{9,11},{10,... | collective-permute-start | bytes 196616 | tf_op jit(solution)/shard_map/ppermute | solution.py:33
  4.9 2.1 %copy-start.3 = (s32[1,2,2,8]{3,2,1,0:T(2,128)S(1)}, s32[1,2,2,8]{3,2,1,0:T(2,128)}, u32[]{:S(2)}) copy-start(s32[1,2,2,8]{3,2,1,0:T(2,128)} %param.13) | copy-start | bytes 388
  4.9 2.1 %copy-start.1 = (bf16[256,2,2,128]{3,2,1,0:T(2,128)(2,1)S(1)}, bf16[256,2,2,128]{3,2,1,0:T(2,128)(2,1)}, u32[]{:S(2)}) copy-start(bf16[256,2,2,128]{3,2,1,0:T(2,128)(2,1)} %param.10) | copy-start | bytes 786436
  5.0 31.7 %collective-permute-start.1 = (bf16[2,4,256,128]{3,2,1,0:T(8,128)(2,1)S(1)}, bf16[2,4,256,128]{3,2,1,0:T(8,128)(2,1)S(1)}, u32[]{:S(2)}, u32[]{:S(2)}) collective-permute-start(bf16[2,4,256,128]{3,2,1,0:T(8,128)(2,1)S(1)} %bitcast.77), channel_id=1, source_target_pairs={{0,1},{1,0},{2,3},{3,2},{4,5},{5,4},{6,7},{7,6},{8,9},{9,8},{10,11... | collective-permute-start | bytes 1572872 | tf_op jit(solution)/shard_map/ppermute | solution.py:33
  8.8 11.9 %collective-permute-start.8 = (bf16[256,128]{1,0:T(8,128)(2,1)S(1)}, bf16[256,128]{1,0:T(8,128)(2,1)S(1)}, u32[]{:S(2)}, u32[]{:S(2)}) collective-permute-start(bf16[256,128]{1,0:T(8,128)(2,1)S(1)} %bitcast.90), channel_id=1, source_target_pairs={{0,192},{16,208},{32,224},{48,240},{1,193},{17,209},{33,225},{49,2... | collective-permute-start | bytes 196616 | tf_op jit(solution)/shard_map/ppermute | solution.py:19
  13.7 7.7 %collective-permute-start.7 = (bf16[256,128]{1,0:T(8,128)(2,1)S(1)}, bf16[256,128]{1,0:T(8,128)(2,1)S(1)}, u32[]{:S(2)}, u32[]{:S(2)}) collective-permute-start(bf16[256,128]{1,0:T(8,128)(2,1)S(1)} %bitcast.91), channel_id=1, source_target_pairs={{0,128},{16,144},{32,160},{48,176},{64,192},{80,208},{96,224},{112... | collective-permute-start | bytes 196616 | tf_op jit(solution)/shard_map/ppermute | solution.py:19
  15.0 7.3 %collective-permute-start.6 = (bf16[256,128]{1,0:T(8,128)(2,1)S(1)}, bf16[256,128]{1,0:T(8,128)(2,1)S(1)}, u32[]{:S(2)}, u32[]{:S(2)}) collective-permute-start(bf16[256,128]{1,0:T(8,128)(2,1)S(1)} %bitcast.92), channel_id=1, source_target_pairs={{0,64},{16,80},{32,96},{48,112},{64,128},{80,144},{96,160},{112,17... | collective-permute-start | bytes 196616 | tf_op jit(solution)/shard_map/ppermute | solution.py:19
  17.8 6.5 %collective-permute-start.5 = (bf16[256,128]{1,0:T(8,128)(2,1)S(1)}, bf16[256,128]{1,0:T(8,128)(2,1)S(1)}, u32[]{:S(2)}, u32[]{:S(2)}) collective-permute-start(bf16[256,128]{1,0:T(8,128)(2,1)S(1)} %bitcast.86), channel_id=1, source_target_pairs={{0,48},{16,0},{32,16},{48,32},{64,112},{80,64},{96,80},{112,96},{1... | collective-permute-start | bytes 196616 | tf_op jit(solution)/shard_map/ppermute | solution.py:19
  20.6 6.5 %collective-permute-start.4 = (bf16[256,128]{1,0:T(8,128)(2,1)S(1)}, bf16[256,128]{1,0:T(8,128)(2,1)S(1)}, u32[]{:S(2)}, u32[]{:S(2)}) collective-permute-start(bf16[256,128]{1,0:T(8,128)(2,1)S(1)} %bitcast.87), channel_id=1, source_target_pairs={{0,32},{16,48},{32,0},{48,16},{64,96},{80,112},{96,64},{112,80},{1... | collective-permute-start | bytes 196616 | tf_op jit(solution)/shard_map/ppermute | solution.py:19
  21.4 6.6 %collective-permute-start.3 = (bf16[256,128]{1,0:T(8,128)(2,1)S(1)}, bf16[256,128]{1,0:T(8,128)(2,1)S(1)}, u32[]{:S(2)}, u32[]{:S(2)}) collective-permute-start(bf16[256,128]{1,0:T(8,128)(2,1)S(1)} %bitcast.88), channel_id=1, source_target_pairs={{0,16},{16,32},{32,48},{48,0},{64,80},{80,96},{96,112},{112,64},{1... | collective-permute-start | bytes 196616 | tf_op jit(solution)/shard_map/ppermute | solution.py:19
  22.4 13.6 %collective-permute-start.11 = (bf16[4,256,128]{2,1,0:T(8,128)(2,1)S(1)}, bf16[4,256,128]{2,1,0:T(8,128)(2,1)S(1)}, u32[]{:S(2)}, u32[]{:S(2)}) collective-permute-start(bf16[4,256,128]{2,1,0:T(8,128)(2,1)S(1)} %pad_maximum_fusion.1.refs_5_), channel_id=1, source_target_pairs={{0,16},{16,32},{32,48},{48,0},{64,80},{80,96},{96,112},{112,64},{1... | collective-permute-start | bytes 786440 | tf_op jit(solution)/shard_map/ppermute | solution.py:19
  28.1 7.9 %collective-permute-start.9 = (bf16[4,256,128]{2,1,0:T(8,128)(2,1)S(1)}, bf16[4,256,128]{2,1,0:T(8,128)(2,1)S(1)}, u32[]{:S(2)}, u32[]{:S(2)}) collective-permute-start(bf16[4,256,128]{2,1,0:T(8,128)(2,1)S(1)} %pad_maximum_fusion.refs_4_), channel_id=1, source_target_pairs={{0,64},{16,80},{32,96},{48,112},{64,128},{80,144},{96,160},{112,17... | collective-permute-start | bytes 786440 | tf_op jit(solution)/shard_map/ppermute | solution.py:19
  30.1 3.8 %collective-permute-start = (f32[3,4,256]{2,1,0:T(4,128)S(1)}, f32[3,4,256]{2,1,0:T(4,128)S(1)}, u32[]{:S(2)}, u32[]{:S(2)}) collective-permute-start(f32[3,4,256]{2,1,0:T(4,128)S(1)} %constant_dynamic-update-slice_fusion), channel_id=1, source_target_pairs={{0,1},{1,0},{2,3},{3,2},{4,5},{5,4},{6,7},{7,6},{8,9},{9,8},{10,11... | collective-permute-start | bytes 36872 | tf_op jit(solution)/shard_map/ppermute | solution.py:33
  30.9 7.8 %collective-permute-start.14 = (bf16[4,256,128]{2,1,0:T(8,128)(2,1)S(1)}, bf16[4,256,128]{2,1,0:T(8,128)(2,1)S(1)}, u32[]{:S(2)}, u32[]{:S(2)}) collective-permute-start(bf16[4,256,128]{2,1,0:T(8,128)(2,1)S(1)} %pad_maximum_fusion.1.refs_5_), channel_id=1, source_target_pairs={{0,48},{16,0},{32,16},{48,32},{64,112},{80,64},{96,80},{112,96},{1... | collective-permute-start | bytes 786440 | tf_op jit(solution)/shard_map/ppermute | solution.py:19
  33.9 5.8 %collective-permute-start.13 = (bf16[4,256,128]{2,1,0:T(8,128)(2,1)S(1)}, bf16[4,256,128]{2,1,0:T(8,128)(2,1)S(1)}, u32[]{:S(2)}, u32[]{:S(2)}) collective-permute-start(bf16[4,256,128]{2,1,0:T(8,128)(2,1)S(1)} %pad_maximum_fusion.refs_4_), channel_id=1, source_target_pairs={{0,192},{16,208},{32,224},{48,240},{1,193},{17,209},{33,225},{49,2... | collective-permute-start | bytes 786440 | tf_op jit(solution)/shard_map/ppermute | solution.py:19
  35.9 7.6 %collective-permute-start.12 = (bf16[4,256,128]{2,1,0:T(8,128)(2,1)S(1)}, bf16[4,256,128]{2,1,0:T(8,128)(2,1)S(1)}, u32[]{:S(2)}, u32[]{:S(2)}) collective-permute-start(bf16[4,256,128]{2,1,0:T(8,128)(2,1)S(1)} %collective-permute-done.11.refs_6_), channel_id=1, source_target_pairs={{0,16},{16,32},{32,48},{48,0},{64,80},{80,96},{96,112},{112,64},{1... | collective-permute-start | bytes 786440 | tf_op jit(solution)/shard_map/ppermute | solution.py:19
  36.0 7.6 %collective-permute-start.10 = (bf16[4,256,128]{2,1,0:T(8,128)(2,1)S(1)}, bf16[4,256,128]{2,1,0:T(8,128)(2,1)S(1)}, u32[]{:S(2)}, u32[]{:S(2)}) collective-permute-start(bf16[4,256,128]{2,1,0:T(8,128)(2,1)S(1)} %collective-permute-done.9.refs_4_), channel_id=1, source_target_pairs={{64,128},{80,144},{96,160},{112,176},{128,192},{144,208},{160,224}... | collective-permute-start | bytes 786440 | tf_op jit(solution)/shard_map/ppermute | solution.py:19
  44.4 6.8 %collective-permute-start.16 = (bf16[4,256,128]{2,1,0:T(8,128)(2,1)S(1)}, bf16[4,256,128]{2,1,0:T(8,128)(2,1)S(1)}, u32[]{:S(2)}, u32[]{:S(2)}) collective-permute-start(bf16[4,256,128]{2,1,0:T(8,128)(2,1)S(1)} %get-tuple-element.27), channel_id=1, source_target_pairs={{128,64},{144,80},{160,96},{176,112},{192,128},{208,144},{224,160}... | collective-permute-start | bytes 786440 | tf_op jit(solution)/shard_map/ppermute | solution.py:19
  45.2 14.6 %collective-permute-start.18 = (bf16[4,256,128]{2,1,0:T(8,128)(2,1)S(1)}, bf16[4,256,128]{2,1,0:T(8,128)(2,1)S(1)}, u32[]{:S(2)}, u32[]{:S(2)}) collective-permute-start(bf16[4,256,128]{2,1,0:T(8,128)(2,1)S(1)} %get-tuple-element.32), channel_id=1, source_target_pairs={{192,0},{208,16},{224,32},{240,48},{193,1},{209,17},{225,33},{241,... | collective-permute-start | bytes 786440 | tf_op jit(solution)/shard_map/ppermute | solution.py:19
  46.5 8.5 %collective-permute-start.22 = (bf16[4,256,128]{2,1,0:T(8,128)(2,1)S(1)}, bf16[4,256,128]{2,1,0:T(8,128)(2,1)S(1)}, u32[]{:S(2)}, u32[]{:S(2)}) collective-permute-start(bf16[4,256,128]{2,1,0:T(8,128)(2,1)S(1)} %get-tuple-element.33), channel_id=1, source_target_pairs={{0,48},{16,0},{32,16},{48,32},{64,112},{80,64},{96,80},{112,96},{1... | collective-permute-start | bytes 786440 | tf_op jit(solution)/shard_map/ppermute | solution.py:19
  51.2 14.6 %collective-permute-start.17 = (bf16[4,256,128]{2,1,0:T(8,128)(2,1)S(1)}, bf16[4,256,128]{2,1,0:T(8,128)(2,1)S(1)}, u32[]{:S(2)}, u32[]{:S(2)}) collective-permute-start(bf16[4,256,128]{2,1,0:T(8,128)(2,1)S(1)} %add_convert_fusion.1), channel_id=1, source_target_pairs={{64,0},{80,16},{96,32},{112,48},{128,64},{144,80},{160,96},{176,11... | collective-permute-start | bytes 786440 | tf_op jit(solution)/shard_map/ppermute | solution.py:19
  52.5 16.6 %collective-permute-start.24 = (bf16[4,256,128]{2,1,0:T(8,128)(2,1)S(1)}, bf16[4,256,128]{2,1,0:T(8,128)(2,1)S(1)}, u32[]{:S(2)}, u32[]{:S(2)}) collective-permute-start(bf16[4,256,128]{2,1,0:T(8,128)(2,1)S(1)} %get-tuple-element.38), channel_id=1, source_target_pairs={{0,16},{16,32},{32,48},{48,0},{64,80},{80,96},{96,112},{112,64},{1... | collective-permute-start | bytes 786440 | tf_op jit(solution)/shard_map/ppermute | solution.py:19
  53.3 28.0 %collective-permute-start.15 = (bf16[4,256,128]{2,1,0:T(8,128)(2,1)S(1)}, bf16[4,256,128]{2,1,0:T(8,128)(2,1)S(1)}, u32[]{:S(2)}, u32[]{:S(2)}) collective-permute-start(bf16[4,256,128]{2,1,0:T(8,128)(2,1)S(1)} %get-tuple-element.26), channel_id=1, source_target_pairs={{0,1},{1,0},{2,3},{3,2},{4,5},{5,4},{6,7},{7,6},{8,9},{9,8},{10,11... | collective-permute-start | bytes 786440 | tf_op jit(solution)/shard_map/ppermute | solution.py:33
  55.1 15.1 %collective-permute-start.23 = (bf16[4,256,128]{2,1,0:T(8,128)(2,1)S(1)}, bf16[4,256,128]{2,1,0:T(8,128)(2,1)S(1)}, u32[]{:S(2)}, u32[]{:S(2)}) collective-permute-start(bf16[4,256,128]{2,1,0:T(8,128)(2,1)S(1)} %add_convert_fusion), channel_id=1, source_target_pairs={{0,48},{16,0},{32,16},{48,32},{64,112},{80,64},{96,80},{112,96},{1... | collective-permute-start | bytes 786440 | tf_op jit(solution)/shard_map/ppermute | solution.py:19
  65.9 5.9 %collective-permute-start.19 = (bf16[256,128]{1,0:T(8,128)(2,1)S(1)}, bf16[256,128]{1,0:T(8,128)(2,1)S(1)}, u32[]{:S(2)}, u32[]{:S(2)}) collective-permute-start(bf16[256,128]{1,0:T(8,128)(2,1)S(1)} %get-tuple-element.43), channel_id=1, source_target_pairs={{0,32},{16,48},{32,0},{48,16},{64,96},{80,112},{96,64},{112,80},{1... | collective-permute-start | bytes 196616 | tf_op jit(solution)/shard_map/ppermute | solution.py:19
  67.0 6.1 %collective-permute-start.21 = (bf16[256,128]{1,0:T(8,128)(2,1)S(1)}, bf16[256,128]{1,0:T(8,128)(2,1)S(1)}, u32[]{:S(2)}, u32[]{:S(2)}) collective-permute-start(bf16[256,128]{1,0:T(8,128)(2,1)S(1)} %get-tuple-element.44), channel_id=1, source_target_pairs={{0,16},{16,32},{32,48},{48,0},{64,80},{80,96},{96,112},{112,64},{1... | collective-permute-start | bytes 196616 | tf_op jit(solution)/shard_map/ppermute | solution.py:19
  69.1 5.2 %collective-permute-start.20 = (bf16[256,128]{1,0:T(8,128)(2,1)S(1)}, bf16[256,128]{1,0:T(8,128)(2,1)S(1)}, u32[]{:S(2)}, u32[]{:S(2)}) collective-permute-start(bf16[256,128]{1,0:T(8,128)(2,1)S(1)} %get-tuple-element.45), channel_id=1, source_target_pairs={{0,48},{16,0},{32,16},{48,32},{64,112},{80,64},{96,80},{112,96},{1... | collective-permute-start | bytes 196616 | tf_op jit(solution)/shard_map/ppermute | solution.py:19
  70.3 7.9 %collective-permute-start.25 = (bf16[256,128]{1,0:T(8,128)(2,1)S(1)}, bf16[256,128]{1,0:T(8,128)(2,1)S(1)}, u32[]{:S(2)}, u32[]{:S(2)}) collective-permute-start(bf16[256,128]{1,0:T(8,128)(2,1)S(1)} %get-tuple-element.46), channel_id=1, source_target_pairs={{128,0},{144,16},{160,32},{176,48},{192,64},{208,80},{224,96},{240... | collective-permute-start | bytes 196616 | tf_op jit(solution)/shard_map/ppermute | solution.py:19
  71.8 9.0 %collective-permute-start.27 = (bf16[256,128]{1,0:T(8,128)(2,1)S(1)}, bf16[256,128]{1,0:T(8,128)(2,1)S(1)}, u32[]{:S(2)}, u32[]{:S(2)}) collective-permute-start(bf16[256,128]{1,0:T(8,128)(2,1)S(1)} %get-tuple-element.47), channel_id=1, source_target_pairs={{192,0},{208,16},{224,32},{240,48},{193,1},{209,17},{225,33},{241,... | collective-permute-start | bytes 196616 | tf_op jit(solution)/shard_map/ppermute | solution.py:19
  73.1 7.7 %collective-permute-start.26 = (bf16[256,128]{1,0:T(8,128)(2,1)S(1)}, bf16[256,128]{1,0:T(8,128)(2,1)S(1)}, u32[]{:S(2)}, u32[]{:S(2)}) collective-permute-start(bf16[256,128]{1,0:T(8,128)(2,1)S(1)} %get-tuple-element.48), channel_id=1, source_target_pairs={{64,0},{80,16},{96,32},{112,48},{128,64},{144,80},{160,96},{176,11... | collective-permute-start | bytes 196616 | tf_op jit(solution)/shard_map/ppermute | solution.py:19
  81.1 6.0 %collective-permute-start.28 = (bf16[2,2,64,128]{3,0,2,1:T(2,128)(2,1)S(1)}, bf16[2,2,64,128]{3,0,2,1:T(2,128)(2,1)S(1)}, u32[]{:S(2)}, u32[]{:S(2)}) collective-permute-start(bf16[2,2,64,128]{3,0,2,1:T(2,128)(2,1)S(1)} %fusion.8), channel_id=1, source_target_pairs={{0,2},{1,3},{2,0},{3,1},{4,6},{5,7},{6,4},{7,5},{8,10},{9,11},{10,... | collective-permute-start | bytes 196616 | tf_op jit(solution)/shard_map/ppermute | solution.py:33
  (1 other events, 0.7 us)

commit v2 on v0

--- a/solution.py
+++ b/solution.py
@@ -44,7 +44,8 @@
     full = jnp.float32
     after = move(after, rows, columns)
     far, own = lax.optimization_barrier((move(far, -rows, -columns), own))
-    before = move((before.astype(full) + far.astype(full)).astype(before.dtype), -rows, -columns)
+    near = (before.astype(full) + far.astype(full)).astype(before.dtype)
+    before = move(near, -rows, -columns)
     return own + before.astype(full) + after.astype(full)
 
 
@@ -296,7 +297,8 @@
     own_0, before_0, after_0, far_0 = gather_large(gather_small(kv[0], 0, 1), 1, 0)
     own_1, before_1, after_1, far_1 = gather_large(gather_small(kv[1], 1, 0), 0, 1)
 
-    delta = jnp.sum(grad_out.astype(full) * forward_out.astype(full), axis=-1).transpose(1, 2, 0)
+    delta = jnp.sum(grad_out.astype(full) * forward_out.astype(full), axis=-1)
+    delta = delta.transpose(1, 2, 0)
     ids = jnp.pad(selected[0].astype(full), ((0, 0), (0, 0), (0, BLOCK - selected.shape[-1])))
     small = jnp.stack([logsumexp, delta, ids]).reshape(3, pairs, BLOCK)
     small_far = swap(small, 1)
@@ -312,7 +314,8 @@
     (far_0, far_1), (dq,) = attend_call(1, *shared, (far_0, far_1), dq, False)
     (own_0, own_1), (dq_own, dq_far) = attend_call(2, *shared, (own_0, own_1), dq, True)
 
-    query_grad = (dq_own + swap(dq_far, 1).astype(full)).astype(low)
+    dq_near = swap(dq_far, 1)
+    query_grad = (dq_own + dq_near.astype(full)).astype(low)
     query_grad = query_grad.reshape(heads, members, rows, head_dim).transpose(2, 0, 1, 3)
 
     grad_0 = reduce_small(reduce_large(own_0, before_0, after_0, far_0, 1, 0), 0, 1)

time: 84 us -> 84 us (level)
  no operation moved by 1% of the time
where the time goes in v2:
time: 84 us; the launch traced here: 82.8 us
  starting transfers between devices  48.9 us (58%)
  waiting for transfers between devices  18.5 us (22%)
  Pallas kernels  7 us (8%)
  local copies, waits for them, and re-layouts  3.73 us (4%)
  other arithmetic  3.7 us (4%)
  between operations  0.9 us (1%)
    ppermute x24, starting transfers between devices, move(): return lax.ppermute(array, 'ctx', shifts(rows, columns))  43.8 us
    ppermute x24, waiting for transfers between devices, move(): return lax.ppermute(array, 'ctx', shifts(rows, columns))  12.2 us
    ppermute x5, waiting for transfers between devices, swap(): return lax.ppermute(array, 'dp', [(d, d ^ bit) for d in range(4)])  6.35 us
    ppermute x5, starting transfers between devices, swap(): return lax.ppermute(array, 'dp', [(d, d ^ bit) for d in range(4)])  5.04 us
    pallas_call x3, Pallas kernels, attend_call(): pl.pallas_call(lambda *refs: attend(*refs, which=which, parts=parts, scal...  4.99 us
    pallas_call x1, Pallas kernels, plan_call(): pl.pallas_call(lambda *refs: plan(*refs, pairs=pairs), out_shape=[jax.Sha...  2.02 us
    transpose x1, other arithmetic, step(): jnp.stack([queries, grad_out]).transpose(0, 2, 3, 1, 4)  1.73 us
  transfers between devices with their start and end apart: 29, of which 12 were waited for; matrix products, arithmetic and copies ran while one was open for 6% of the time, Pallas kernels for 7%

profile of v2, /device:TPU:0, one launch (start us, length us, event | category | flops | bytes accessed | tf_op | source)
XLA Modules:
  0.0 82.8 jit_solution(12229106713565512849)
XLA Ops:
  1.5 1.6 %collective-permute-start.2 = (bf16[2,2,64,128]{3,2,1,0:T(8,128)(2,1)S(1)}, bf16[2,2,64,128]{3,2,1,0:T(8,128)(2,1)S(1)}, u32[]{:S(2)}, u32[]{:S(2)}) collective-permute-start(bf16[2,2,64,128]{3,2,1,0:T(8,128)(2,1)S(1)} %maximum_bitcast_fusion.1), channel_id=1, source_target_pairs={{0,2},{1,3},{2,0},{3,1},{4,6},{5,7},{6,4},{7,5},{8,10},{9,11},{10,... | collective-permute-start | bytes 196616 | tf_op jit(solution)/shard_map/ppermute | solution.py:26
  3.1 1.7 %maximum_bitcast_fusion = bf16[2,2,2,256,128]{4,2,1,3,0:T(2,128)(2,1)S(1)} fusion(bf16[1,256,2,2,128]{4,3,2,1,0:T(2,128)(2,1)S(1)} %bitcast.80, bf16[1,256,2,2,128]{4,3,2,1,0:T(2,128)(2,1)} %bitcast.85), kind=kLoop, calls=%fused_computation | loop fusion | flops 262144 | bytes 1048576 | tf_op jit(solution)/shard_map/transpose | solution.py:294
  5.0 2.0 %collective-permute-start.1 = (bf16[2,4,256,128]{3,2,1,0:T(8,128)(2,1)S(1)}, bf16[2,4,256,128]{3,2,1,0:T(8,128)(2,1)S(1)}, u32[]{:S(2)}, u32[]{:S(2)}) collective-permute-start(bf16[2,4,256,128]{3,2,1,0:T(8,128)(2,1)S(1)} %bitcast.77), channel_id=1, source_target_pairs={{0,1},{1,0},{2,3},{3,2},{4,5},{5,4},{6,7},{7,6},{8,9},{9,8},{10,11... | collective-permute-start | bytes 1572872 | tf_op jit(solution)/shard_map/ppermute | solution.py:26
  8.8 3.1 %collective-permute-start.8 = (bf16[256,128]{1,0:T(8,128)(2,1)S(1)}, bf16[256,128]{1,0:T(8,128)(2,1)S(1)}, u32[]{:S(2)}, u32[]{:S(2)}) collective-permute-start(bf16[256,128]{1,0:T(8,128)(2,1)S(1)} %bitcast.90), channel_id=1, source_target_pairs={{0,192},{16,208},{32,224},{48,240},{64,0},{80,16},{96,32},{112,48}... | collective-permute-start | bytes 196616 | tf_op jit(solution)/shard_map/ppermute | solution.py:22
  13.5 2.8 %collective-permute-start.5 = (bf16[256,128]{1,0:T(8,128)(2,1)S(1)}, bf16[256,128]{1,0:T(8,128)(2,1)S(1)}, u32[]{:S(2)}, u32[]{:S(2)}) collective-permute-start(bf16[256,128]{1,0:T(8,128)(2,1)S(1)} %bitcast.86), channel_id=1, source_target_pairs={{0,48},{16,0},{32,16},{48,32},{64,112},{80,64},{96,80},{112,96},{1... | collective-permute-start | bytes 196616 | tf_op jit(solution)/shard_map/ppermute | solution.py:22
  17.7 1.5 %collective-permute-start.3 = (bf16[256,128]{1,0:T(8,128)(2,1)S(1)}, bf16[256,128]{1,0:T(8,128)(2,1)S(1)}, u32[]{:S(2)}, u32[]{:S(2)}) collective-permute-start(bf16[256,128]{1,0:T(8,128)(2,1)S(1)} %bitcast.88), channel_id=1, source_target_pairs={{0,16},{16,32},{32,48},{48,0},{64,80},{80,96},{96,112},{112,64},{1... | collective-permute-start | bytes 196616 | tf_op jit(solution)/shard_map/ppermute | solution.py:22
  19.2 1.6 %collective-permute-start.11 = (bf16[4,256,128]{2,1,0:T(8,128)(2,1)S(1)}, bf16[4,256,128]{2,1,0:T(8,128)(2,1)S(1)}, u32[]{:S(2)}, u32[]{:S(2)}) collective-permute-start(bf16[4,256,128]{2,1,0:T(8,128)(2,1)S(1)} %pad_maximum_fusion.1.refs_5_), channel_id=1, source_target_pairs={{0,16},{16,32},{32,48},{48,0},{64,80},{80,96},{96,112},{112,64},{1... | collective-permute-start | bytes 786440 | tf_op jit(solution)/shard_map/ppermute | solution.py:22
  20.8 1.9 %collective-permute-done.4 = bf16[256,128]{1,0:T(8,128)(2,1)S(1)} collective-permute-done((bf16[256,128]{1,0:T(8,128)(2,1)S(1)}, bf16[256,128]{1,0:T(8,128)(2,1)S(1)}, u32[]{:S(2)}, u32[]{:S(2)}) %collective-permute-start.4) | collective-permute-done | bytes 65568 | tf_op jit(solution)/shard_map/ppermute | solution.py:22
  22.7 1.3 %collective-permute-done.3 = bf16[256,128]{1,0:T(8,128)(2,1)S(1)} collective-permute-done((bf16[256,128]{1,0:T(8,128)(2,1)S(1)}, bf16[256,128]{1,0:T(8,128)(2,1)S(1)}, u32[]{:S(2)}, u32[]{:S(2)}) %collective-permute-start.3) | collective-permute-done | bytes 65568 | tf_op jit(solution)/shard_map/ppermute | solution.py:22
  24.0 1.6 %collective-permute-start.9 = (bf16[4,256,128]{2,1,0:T(8,128)(2,1)S(1)}, bf16[4,256,128]{2,1,0:T(8,128)(2,1)S(1)}, u32[]{:S(2)}, u32[]{:S(2)}) collective-permute-start(bf16[4,256,128]{2,1,0:T(8,128)(2,1)S(1)} %pad_maximum_fusion.refs_4_), channel_id=1, source_target_pairs={{0,64},{16,80},{32,96},{48,112},{64,128},{80,144},{96,160},{112,17... | collective-permute-start | bytes 786440 | tf_op jit(solution)/shard_map/ppermute | solution.py:22
  26.5 1.0 %collective-permute-start.14 = (bf16[4,256,128]{2,1,0:T(8,128)(2,1)S(1)}, bf16[4,256,128]{2,1,0:T(8,128)(2,1)S(1)}, u32[]{:S(2)}, u32[]{:S(2)}) collective-permute-start(bf16[4,256,128]{2,1,0:T(8,128)(2,1)S(1)} %pad_maximum_fusion.1.refs_5_), channel_id=1, source_target_pairs={{0,48},{16,0},{32,16},{48,32},{64,112},{80,64},{96,80},{112,96},{1... | collective-permute-start | bytes 786440 | tf_op jit(solution)/shard_map/ppermute | solution.py:22
  27.6 1.9 %collective-permute-done = f32[3,4,256]{2,1,0:T(4,128)S(1)} collective-permute-done((f32[3,4,256]{2,1,0:T(4,128)S(1)}, f32[3,4,256]{2,1,0:T(4,128)S(1)}, u32[]{:S(2)}, u32[]{:S(2)}) %collective-permute-start) | collective-permute-done | bytes 12320 | tf_op jit(solution)/shard_map/ppermute | solution.py:26
  29.5 1.7 %collective-permute-start.13 = (bf16[4,256,128]{2,1,0:T(8,128)(2,1)S(1)}, bf16[4,256,128]{2,1,0:T(8,128)(2,1)S(1)}, u32[]{:S(2)}, u32[]{:S(2)}) collective-permute-start(bf16[4,256,128]{2,1,0:T(8,128)(2,1)S(1)} %pad_maximum_fusion.refs_4_), channel_id=1, source_target_pairs={{0,192},{16,208},{32,224},{48,240},{64,0},{80,16},{96,32},{112,48}... | collective-permute-start | bytes 786440 | tf_op jit(solution)/shard_map/ppermute | solution.py:22
  31.4 1.4 %collective-permute-done.9.refs_4_ = bf16[4,256,128]{2,1,0:T(8,128)(2,1)S(1)} collective-permute-done((bf16[4,256,128]{2,1,0:T(8,128)(2,1)S(1)}, bf16[4,256,128]{2,1,0:T(8,128)(2,1)S(1)}, u32[]{:S(2)}, u32[]{:S(2)}) %collective-permute-start.9) | collective-permute-done | bytes 262176 | tf_op jit(solution)/shard_map/ppermute | solution.py:22
  32.8 1.4 %collective-permute-start.10 = (bf16[4,256,128]{2,1,0:T(8,128)(2,1)S(1)}, bf16[4,256,128]{2,1,0:T(8,128)(2,1)S(1)}, u32[]{:S(2)}, u32[]{:S(2)}) collective-permute-start(bf16[4,256,128]{2,1,0:T(8,128)(2,1)S(1)} %collective-permute-done.9.refs_4_), channel_id=1, source_target_pairs={{0,64},{16,80},{32,96},{48,112},{64,128},{80,144},{96,160},{112,17... | collective-permute-start | bytes 786440 | tf_op jit(solution)/shard_map/ppermute | solution.py:22
  34.3 2.0 %plan.1 = (s32[720]{0:T(1024)S(1)}, bf16[2,8,256,128]{3,2,1,0:T(8,128)(2,1)S(1)}) custom-call(s32[8,8]{1,0:T(8,128)S(1)} %fusion.10.refs_0_, s32[3]{0:T(128)S(1)} %pad_add_fusion.refs_1_, bf16[2,4,256,128]{3,2,1,0:T(8,128)(2,1)S(1)} %bitcast.78, bf16[2,4,256,128]{3,2,1,0:T(8,128)(2,1)S(1)} %collective-permute-done.1.refs_3_), custom_call_target="tpu_custom_call" | custom-call | flops 1048576 | bytes 4194304 | tf_op jit(solution)/shard_map/plan/pallas_call | solution.py:108
  37.3 1.5 %collective-permute-done.12.refs_5_ = bf16[4,256,128]{2,1,0:T(8,128)(2,1)S(1)} collective-permute-done((bf16[4,256,128]{2,1,0:T(8,128)(2,1)S(1)}, bf16[4,256,128]{2,1,0:T(8,128)(2,1)S(1)}, u32[]{:S(2)}, u32[]{:S(2)}) %collective-permute-start.12) | collective-permute-done | bytes 262176 | tf_op jit(solution)/shard_map/ppermute | solution.py:22
  38.8 1.6 %collective-permute-done.10.refs_4_ = bf16[4,256,128]{2,1,0:T(8,128)(2,1)S(1)} collective-permute-done((bf16[4,256,128]{2,1,0:T(8,128)(2,1)S(1)}, bf16[4,256,128]{2,1,0:T(8,128)(2,1)S(1)}, u32[]{:S(2)}, u32[]{:S(2)}) %collective-permute-start.10) | collective-permute-done | bytes 262176 | tf_op jit(solution)/shard_map/ppermute | solution.py:22
  41.2 6.7 %collective-permute-start.16 = (bf16[4,256,128]{2,1,0:T(8,128)(2,1)S(1)}, bf16[4,256,128]{2,1,0:T(8,128)(2,1)S(1)}, u32[]{:S(2)}, u32[]{:S(2)}) collective-permute-start(bf16[4,256,128]{2,1,0:T(8,128)(2,1)S(1)} %get-tuple-element.27), channel_id=1, source_target_pairs={{0,192},{16,208},{32,224},{48,240},{64,0},{80,16},{96,32},{112,48}... | collective-permute-start | bytes 786440 | tf_op jit(solution)/shard_map/ppermute | solution.py:22
  47.9 1.4 %collective-permute-start.22 = (bf16[4,256,128]{2,1,0:T(8,128)(2,1)S(1)}, bf16[4,256,128]{2,1,0:T(8,128)(2,1)S(1)}, u32[]{:S(2)}, u32[]{:S(2)}) collective-permute-start(bf16[4,256,128]{2,1,0:T(8,128)(2,1)S(1)} %get-tuple-element.33), channel_id=1, source_target_pairs={{0,48},{16,0},{32,16},{48,32},{64,112},{80,64},{96,80},{112,96},{1... | collective-permute-start | bytes 786440 | tf_op jit(solution)/shard_map/ppermute | solution.py:22
  49.4 3.2 %shard_map.96 = (f32[4,256,128]{2,1,0:T(8,128)S(1)}, f32[4,256,128]{2,1,0:T(8,128)S(1)}, f32[4,256,128]{2,1,0:T(8,128)S(1)}, bf16[4,256,128]{2,1,0:T(8,128)(2,1)S(1)}) custom-call(s32[720]{0:T(1024)S(1)} %get-tuple-element.21.refs_0_, s32[3]{0:T(128)S(1)} %pad_add_fusion.refs_1_, f32[16,256]{1,0:T(8,128)S(1)} %fusion.9.refs_2_, ...), custom_call_target="tpu_custom_call" | custom-call | flops 671088640 | bytes 6291456 | tf_op jit(solution)/shard_map/pallas_call | solution.py:258
  53.5 3.8 %collective-permute-start.17 = (bf16[4,256,128]{2,1,0:T(8,128)(2,1)S(1)}, bf16[4,256,128]{2,1,0:T(8,128)(2,1)S(1)}, u32[]{:S(2)}, u32[]{:S(2)}) collective-permute-start(bf16[4,256,128]{2,1,0:T(8,128)(2,1)S(1)} %add_convert_fusion.1), channel_id=1, source_target_pairs={{0,192},{16,208},{32,224},{48,240},{64,0},{80,16},{96,32},{112,48}... | collective-permute-start | bytes 786440 | tf_op jit(solution)/shard_map/ppermute | solution.py:22
  57.9 3.2 %collective-permute-start.23 = (bf16[4,256,128]{2,1,0:T(8,128)(2,1)S(1)}, bf16[4,256,128]{2,1,0:T(8,128)(2,1)S(1)}, u32[]{:S(2)}, u32[]{:S(2)}) collective-permute-start(bf16[4,256,128]{2,1,0:T(8,128)(2,1)S(1)} %add_convert_fusion), channel_id=1, source_target_pairs={{0,48},{16,0},{32,16},{48,32},{64,112},{80,64},{96,80},{112,96},{1... | collective-permute-start | bytes 786440 | tf_op jit(solution)/shard_map/ppermute | solution.py:22
  61.2 2.4 %collective-permute-start.19 = (bf16[256,128]{1,0:T(8,128)(2,1)S(1)}, bf16[256,128]{1,0:T(8,128)(2,1)S(1)}, u32[]{:S(2)}, u32[]{:S(2)}) collective-permute-start(bf16[256,128]{1,0:T(8,128)(2,1)S(1)} %get-tuple-element.43), channel_id=1, source_target_pairs={{0,32},{16,48},{32,0},{48,16},{64,96},{80,112},{96,64},{112,80},{1... | collective-permute-start | bytes 196616 | tf_op jit(solution)/shard_map/ppermute | solution.py:22
  63.6 1.9 %collective-permute-start.21 = (bf16[256,128]{1,0:T(8,128)(2,1)S(1)}, bf16[256,128]{1,0:T(8,128)(2,1)S(1)}, u32[]{:S(2)}, u32[]{:S(2)}) collective-permute-start(bf16[256,128]{1,0:T(8,128)(2,1)S(1)} %get-tuple-element.44), channel_id=1, source_target_pairs={{0,16},{16,32},{32,48},{48,0},{64,80},{80,96},{96,112},{112,64},{1... | collective-permute-start | bytes 196616 | tf_op jit(solution)/shard_map/ppermute | solution.py:22
  65.5 1.3 %collective-permute-start.20 = (bf16[256,128]{1,0:T(8,128)(2,1)S(1)}, bf16[256,128]{1,0:T(8,128)(2,1)S(1)}, u32[]{:S(2)}, u32[]{:S(2)}) collective-permute-start(bf16[256,128]{1,0:T(8,128)(2,1)S(1)} %get-tuple-element.45), channel_id=1, source_target_pairs={{0,48},{16,0},{32,16},{48,32},{64,112},{80,64},{96,80},{112,96},{1... | collective-permute-start | bytes 196616 | tf_op jit(solution)/shard_map/ppermute | solution.py:22
  67.0 2.0 %collective-permute-start.25 = (bf16[256,128]{1,0:T(8,128)(2,1)S(1)}, bf16[256,128]{1,0:T(8,128)(2,1)S(1)}, u32[]{:S(2)}, u32[]{:S(2)}) collective-permute-start(bf16[256,128]{1,0:T(8,128)(2,1)S(1)} %get-tuple-element.46), channel_id=1, source_target_pairs={{0,128},{16,144},{32,160},{48,176},{64,192},{80,208},{96,224},{112... | collective-permute-start | bytes 196616 | tf_op jit(solution)/shard_map/ppermute | solution.py:22
  69.0 2.6 %collective-permute-start.27 = (bf16[256,128]{1,0:T(8,128)(2,1)S(1)}, bf16[256,128]{1,0:T(8,128)(2,1)S(1)}, u32[]{:S(2)}, u32[]{:S(2)}) collective-permute-start(bf16[256,128]{1,0:T(8,128)(2,1)S(1)} %get-tuple-element.47), channel_id=1, source_target_pairs={{0,64},{16,80},{32,96},{48,112},{64,128},{80,144},{96,160},{112,17... | collective-permute-start | bytes 196616 | tf_op jit(solution)/shard_map/ppermute | solution.py:22
  71.6 1.2 %collective-permute-start.26 = (bf16[256,128]{1,0:T(8,128)(2,1)S(1)}, bf16[256,128]{1,0:T(8,128)(2,1)S(1)}, u32[]{:S(2)}, u32[]{:S(2)}) collective-permute-start(bf16[256,128]{1,0:T(8,128)(2,1)S(1)} %get-tuple-element.48), channel_id=1, source_target_pairs={{0,192},{16,208},{32,224},{48,240},{64,0},{80,16},{96,32},{112,48}... | collective-permute-start | bytes 196616 | tf_op jit(solution)/shard_map/ppermute | solution.py:22
  73.0 1.5 %collective-permute-done.27 = bf16[256,128]{1,0:T(8,128)(2,1)S(1)} collective-permute-done((bf16[256,128]{1,0:T(8,128)(2,1)S(1)}, bf16[256,128]{1,0:T(8,128)(2,1)S(1)}, u32[]{:S(2)}, u32[]{:S(2)}) %collective-permute-start.27) | collective-permute-done | bytes 65568 | tf_op jit(solution)/shard_map/ppermute | solution.py:22
  74.5 1.4 %collective-permute-done.26 = bf16[256,128]{1,0:T(8,128)(2,1)S(1)} collective-permute-done((bf16[256,128]{1,0:T(8,128)(2,1)S(1)}, bf16[256,128]{1,0:T(8,128)(2,1)S(1)}, u32[]{:S(2)}, u32[]{:S(2)}) %collective-permute-start.26) | collective-permute-done | bytes 65568 | tf_op jit(solution)/shard_map/ppermute | solution.py:22
  77.4 4.4 %collective-permute-done.28 = bf16[2,2,64,128]{3,0,2,1:T(2,128)(2,1)S(1)} collective-permute-done((bf16[2,2,64,128]{3,0,2,1:T(2,128)(2,1)S(1)}, bf16[2,2,64,128]{3,0,2,1:T(2,128)(2,1)S(1)}, u32[]{:S(2)}, u32[]{:S(2)}) %collective-permute-start.28) | collective-permute-done | bytes 65568 | tf_op jit(solution)/shard_map/ppermute | solution.py:26
  (74 shorter events, 13.1 us)
Async XLA Ops:
  0.6 2.5 %copy-start = (bf16[256,2,2,128]{3,2,1,0:T(2,128)(2,1)S(1)}, bf16[256,2,2,128]{3,2,1,0:T(2,128)(2,1)}, u32[]{:S(2)}) copy-start(bf16[256,2,2,128]{3,2,1,0:T(2,128)(2,1)} %param.11) | copy-start | bytes 786436
  1.5 7.2 %collective-permute-start.2 = (bf16[2,2,64,128]{3,2,1,0:T(8,128)(2,1)S(1)}, bf16[2,2,64,128]{3,2,1,0:T(8,128)(2,1)S(1)}, u32[]{:S(2)}, u32[]{:S(2)}) collective-permute-start(bf16[2,2,64,128]{3,2,1,0:T(8,128)(2,1)S(1)} %maximum_bitcast_fusion.1), channel_id=1, source_target_pairs={{0,2},{1,3},{2,0},{3,1},{4,6},{5,7},{6,4},{7,5},{8,10},{9,11},{10,... | collective-permute-start | bytes 196616 | tf_op jit(solution)/shard_map/ppermute | solution.py:26
  4.9 2.1 %copy-start.3 = (s32[1,2,2,8]{3,2,1,0:T(2,128)S(1)}, s32[1,2,2,8]{3,2,1,0:T(2,128)}, u32[]{:S(2)}) copy-start(s32[1,2,2,8]{3,2,1,0:T(2,128)} %param.13) | copy-start | bytes 388
  4.9 2.1 %copy-start.1 = (bf16[256,2,2,128]{3,2,1,0:T(2,128)(2,1)S(1)}, bf16[256,2,2,128]{3,2,1,0:T(2,128)(2,1)}, u32[]{:S(2)}) copy-start(bf16[256,2,2,128]{3,2,1,0:T(2,128)(2,1)} %param.10) | copy-start | bytes 786436
  5.0 29.3 %collective-permute-start.1 = (bf16[2,4,256,128]{3,2,1,0:T(8,128)(2,1)S(1)}, bf16[2,4,256,128]{3,2,1,0:T(8,128)(2,1)S(1)}, u32[]{:S(2)}, u32[]{:S(2)}) collective-permute-start(bf16[2,4,256,128]{3,2,1,0:T(8,128)(2,1)S(1)} %bitcast.77), channel_id=1, source_target_pairs={{0,1},{1,0},{2,3},{3,2},{4,5},{5,4},{6,7},{7,6},{8,9},{9,8},{10,11... | collective-permute-start | bytes 1572872 | tf_op jit(solution)/shard_map/ppermute | solution.py:26
  8.8 7.5 %collective-permute-start.8 = (bf16[256,128]{1,0:T(8,128)(2,1)S(1)}, bf16[256,128]{1,0:T(8,128)(2,1)S(1)}, u32[]{:S(2)}, u32[]{:S(2)}) collective-permute-start(bf16[256,128]{1,0:T(8,128)(2,1)S(1)} %bitcast.90), channel_id=1, source_target_pairs={{0,192},{16,208},{32,224},{48,240},{64,0},{80,16},{96,32},{112,48}... | collective-permute-start | bytes 196616 | tf_op jit(solution)/shard_map/ppermute | solution.py:22
  11.9 5.8 %collective-permute-start.7 = (bf16[256,128]{1,0:T(8,128)(2,1)S(1)}, bf16[256,128]{1,0:T(8,128)(2,1)S(1)}, u32[]{:S(2)}, u32[]{:S(2)}) collective-permute-start(bf16[256,128]{1,0:T(8,128)(2,1)S(1)} %bitcast.91), channel_id=1, source_target_pairs={{0,128},{16,144},{32,160},{48,176},{64,192},{80,208},{96,224},{112... | collective-permute-start | bytes 196616 | tf_op jit(solution)/shard_map/ppermute | solution.py:22
  12.5 6.7 %collective-permute-start.6 = (bf16[256,128]{1,0:T(8,128)(2,1)S(1)}, bf16[256,128]{1,0:T(8,128)(2,1)S(1)}, u32[]{:S(2)}, u32[]{:S(2)}) collective-permute-start(bf16[256,128]{1,0:T(8,128)(2,1)S(1)} %bitcast.92), channel_id=1, source_target_pairs={{0,64},{16,80},{32,96},{48,112},{64,128},{80,144},{96,160},{112,17... | collective-permute-start | bytes 196616 | tf_op jit(solution)/shard_map/ppermute | solution.py:22
  13.5 7.3 %collective-permute-start.5 = (bf16[256,128]{1,0:T(8,128)(2,1)S(1)}, bf16[256,128]{1,0:T(8,128)(2,1)S(1)}, u32[]{:S(2)}, u32[]{:S(2)}) collective-permute-start(bf16[256,128]{1,0:T(8,128)(2,1)S(1)} %bitcast.86), channel_id=1, source_target_pairs={{0,48},{16,0},{32,16},{48,32},{64,112},{80,64},{96,80},{112,96},{1... | collective-permute-start | bytes 196616 | tf_op jit(solution)/shard_map/ppermute | solution.py:22
  16.2 6.5 %collective-permute-start.4 = (bf16[256,128]{1,0:T(8,128)(2,1)S(1)}, bf16[256,128]{1,0:T(8,128)(2,1)S(1)}, u32[]{:S(2)}, u32[]{:S(2)}) collective-permute-start(bf16[256,128]{1,0:T(8,128)(2,1)S(1)} %bitcast.87), channel_id=1, source_target_pairs={{0,32},{16,48},{32,0},{48,16},{64,96},{80,112},{96,64},{112,80},{1... | collective-permute-start | bytes 196616 | tf_op jit(solution)/shard_map/ppermute | solution.py:22
  17.7 6.3 %collective-permute-start.3 = (bf16[256,128]{1,0:T(8,128)(2,1)S(1)}, bf16[256,128]{1,0:T(8,128)(2,1)S(1)}, u32[]{:S(2)}, u32[]{:S(2)}) collective-permute-start(bf16[256,128]{1,0:T(8,128)(2,1)S(1)} %bitcast.88), channel_id=1, source_target_pairs={{0,16},{16,32},{32,48},{48,0},{64,80},{80,96},{96,112},{112,64},{1... | collective-permute-start | bytes 196616 | tf_op jit(solution)/shard_map/ppermute | solution.py:22
  19.2 12.0 %collective-permute-start.11 = (bf16[4,256,128]{2,1,0:T(8,128)(2,1)S(1)}, bf16[4,256,128]{2,1,0:T(8,128)(2,1)S(1)}, u32[]{:S(2)}, u32[]{:S(2)}) collective-permute-start(bf16[4,256,128]{2,1,0:T(8,128)(2,1)S(1)} %pad_maximum_fusion.1.refs_5_), channel_id=1, source_target_pairs={{0,16},{16,32},{32,48},{48,0},{64,80},{80,96},{96,112},{112,64},{1... | collective-permute-start | bytes 786440 | tf_op jit(solution)/shard_map/ppermute | solution.py:22
  24.0 8.8 %collective-permute-start.9 = (bf16[4,256,128]{2,1,0:T(8,128)(2,1)S(1)}, bf16[4,256,128]{2,1,0:T(8,128)(2,1)S(1)}, u32[]{:S(2)}, u32[]{:S(2)}) collective-permute-start(bf16[4,256,128]{2,1,0:T(8,128)(2,1)S(1)} %pad_maximum_fusion.refs_4_), channel_id=1, source_target_pairs={{0,64},{16,80},{32,96},{48,112},{64,128},{80,144},{96,160},{112,17... | collective-permute-start | bytes 786440 | tf_op jit(solution)/shard_map/ppermute | solution.py:22
  25.7 3.8 %collective-permute-start = (f32[3,4,256]{2,1,0:T(4,128)S(1)}, f32[3,4,256]{2,1,0:T(4,128)S(1)}, u32[]{:S(2)}, u32[]{:S(2)}) collective-permute-start(f32[3,4,256]{2,1,0:T(4,128)S(1)} %constant_dynamic-update-slice_fusion), channel_id=1, source_target_pairs={{0,1},{1,0},{2,3},{3,2},{4,5},{5,4},{6,7},{7,6},{8,9},{9,8},{10,11... | collective-permute-start | bytes 36872 | tf_op jit(solution)/shard_map/ppermute | solution.py:26
  26.5 9.7 %collective-permute-start.14 = (bf16[4,256,128]{2,1,0:T(8,128)(2,1)S(1)}, bf16[4,256,128]{2,1,0:T(8,128)(2,1)S(1)}, u32[]{:S(2)}, u32[]{:S(2)}) collective-permute-start(bf16[4,256,128]{2,1,0:T(8,128)(2,1)S(1)} %pad_maximum_fusion.1.refs_5_), channel_id=1, source_target_pairs={{0,48},{16,0},{32,16},{48,32},{64,112},{80,64},{96,80},{112,96},{1... | collective-permute-start | bytes 786440 | tf_op jit(solution)/shard_map/ppermute | solution.py:22
  29.5 6.8 %collective-permute-start.13 = (bf16[4,256,128]{2,1,0:T(8,128)(2,1)S(1)}, bf16[4,256,128]{2,1,0:T(8,128)(2,1)S(1)}, u32[]{:S(2)}, u32[]{:S(2)}) collective-permute-start(bf16[4,256,128]{2,1,0:T(8,128)(2,1)S(1)} %pad_maximum_fusion.refs_4_), channel_id=1, source_target_pairs={{0,192},{16,208},{32,224},{48,240},{64,0},{80,16},{96,32},{112,48}... | collective-permute-start | bytes 786440 | tf_op jit(solution)/shard_map/ppermute | solution.py:22
  31.2 7.6 %collective-permute-start.12 = (bf16[4,256,128]{2,1,0:T(8,128)(2,1)S(1)}, bf16[4,256,128]{2,1,0:T(8,128)(2,1)S(1)}, u32[]{:S(2)}, u32[]{:S(2)}) collective-permute-start(bf16[4,256,128]{2,1,0:T(8,128)(2,1)S(1)} %collective-permute-done.11.refs_6_), channel_id=1, source_target_pairs={{0,16},{16,32},{32,48},{48,0},{64,80},{80,96},{96,112},{112,64},{1... | collective-permute-start | bytes 786440 | tf_op jit(solution)/shard_map/ppermute | solution.py:22
  32.8 7.6 %collective-permute-start.10 = (bf16[4,256,128]{2,1,0:T(8,128)(2,1)S(1)}, bf16[4,256,128]{2,1,0:T(8,128)(2,1)S(1)}, u32[]{:S(2)}, u32[]{:S(2)}) collective-permute-start(bf16[4,256,128]{2,1,0:T(8,128)(2,1)S(1)} %collective-permute-done.9.refs_4_), channel_id=1, source_target_pairs={{0,64},{16,80},{32,96},{48,112},{64,128},{80,144},{96,160},{112,17... | collective-permute-start | bytes 786440 | tf_op jit(solution)/shard_map/ppermute | solution.py:22
  41.2 12.2 %collective-permute-start.16 = (bf16[4,256,128]{2,1,0:T(8,128)(2,1)S(1)}, bf16[4,256,128]{2,1,0:T(8,128)(2,1)S(1)}, u32[]{:S(2)}, u32[]{:S(2)}) collective-permute-start(bf16[4,256,128]{2,1,0:T(8,128)(2,1)S(1)} %get-tuple-element.27), channel_id=1, source_target_pairs={{0,192},{16,208},{32,224},{48,240},{64,0},{80,16},{96,32},{112,48}... | collective-permute-start | bytes 786440 | tf_op jit(solution)/shard_map/ppermute | solution.py:22
  47.9 13.1 %collective-permute-start.18 = (bf16[4,256,128]{2,1,0:T(8,128)(2,1)S(1)}, bf16[4,256,128]{2,1,0:T(8,128)(2,1)S(1)}, u32[]{:S(2)}, u32[]{:S(2)}) collective-permute-start(bf16[4,256,128]{2,1,0:T(8,128)(2,1)S(1)} %get-tuple-element.32), channel_id=1, source_target_pairs={{0,64},{16,80},{32,96},{48,112},{64,128},{80,144},{96,160},{112,17... | collective-permute-start | bytes 786440 | tf_op jit(solution)/shard_map/ppermute | solution.py:22
  47.9 9.9 %collective-permute-start.22 = (bf16[4,256,128]{2,1,0:T(8,128)(2,1)S(1)}, bf16[4,256,128]{2,1,0:T(8,128)(2,1)S(1)}, u32[]{:S(2)}, u32[]{:S(2)}) collective-permute-start(bf16[4,256,128]{2,1,0:T(8,128)(2,1)S(1)} %get-tuple-element.33), channel_id=1, source_target_pairs={{0,48},{16,0},{32,16},{48,32},{64,112},{80,64},{96,80},{112,96},{1... | collective-permute-start | bytes 786440 | tf_op jit(solution)/shard_map/ppermute | solution.py:22
  53.5 7.7 %collective-permute-start.17 = (bf16[4,256,128]{2,1,0:T(8,128)(2,1)S(1)}, bf16[4,256,128]{2,1,0:T(8,128)(2,1)S(1)}, u32[]{:S(2)}, u32[]{:S(2)}) collective-permute-start(bf16[4,256,128]{2,1,0:T(8,128)(2,1)S(1)} %add_convert_fusion.1), channel_id=1, source_target_pairs={{0,192},{16,208},{32,224},{48,240},{64,0},{80,16},{96,32},{112,48}... | collective-permute-start | bytes 786440 | tf_op jit(solution)/shard_map/ppermute | solution.py:22
  57.2 8.3 %collective-permute-start.24 = (bf16[4,256,128]{2,1,0:T(8,128)(2,1)S(1)}, bf16[4,256,128]{2,1,0:T(8,128)(2,1)S(1)}, u32[]{:S(2)}, u32[]{:S(2)}) collective-permute-start(bf16[4,256,128]{2,1,0:T(8,128)(2,1)S(1)} %get-tuple-element.38), channel_id=1, source_target_pairs={{0,16},{16,32},{32,48},{48,0},{64,80},{80,96},{96,112},{112,64},{1... | collective-permute-start | bytes 786440 | tf_op jit(solution)/shard_map/ppermute | solution.py:22
  57.4 19.0 %collective-permute-start.15 = (bf16[4,256,128]{2,1,0:T(8,128)(2,1)S(1)}, bf16[4,256,128]{2,1,0:T(8,128)(2,1)S(1)}, u32[]{:S(2)}, u32[]{:S(2)}) collective-permute-start(bf16[4,256,128]{2,1,0:T(8,128)(2,1)S(1)} %get-tuple-element.26), channel_id=1, source_target_pairs={{0,1},{1,0},{2,3},{3,2},{4,5},{5,4},{6,7},{7,6},{8,9},{9,8},{10,11... | collective-permute-start | bytes 786440 | tf_op jit(solution)/shard_map/ppermute | solution.py:26
  57.9 9.0 %collective-permute-start.23 = (bf16[4,256,128]{2,1,0:T(8,128)(2,1)S(1)}, bf16[4,256,128]{2,1,0:T(8,128)(2,1)S(1)}, u32[]{:S(2)}, u32[]{:S(2)}) collective-permute-start(bf16[4,256,128]{2,1,0:T(8,128)(2,1)S(1)} %add_convert_fusion), channel_id=1, source_target_pairs={{0,48},{16,0},{32,16},{48,32},{64,112},{80,64},{96,80},{112,96},{1... | collective-permute-start | bytes 786440 | tf_op jit(solution)/shard_map/ppermute | solution.py:22
  61.2 7.8 %collective-permute-start.19 = (bf16[256,128]{1,0:T(8,128)(2,1)S(1)}, bf16[256,128]{1,0:T(8,128)(2,1)S(1)}, u32[]{:S(2)}, u32[]{:S(2)}) collective-permute-start(bf16[256,128]{1,0:T(8,128)(2,1)S(1)} %get-tuple-element.43), channel_id=1, source_target_pairs={{0,32},{16,48},{32,0},{48,16},{64,96},{80,112},{96,64},{112,80},{1... | collective-permute-start | bytes 196616 | tf_op jit(solution)/shard_map/ppermute | solution.py:22
  63.6 8.0 %collective-permute-start.21 = (bf16[256,128]{1,0:T(8,128)(2,1)S(1)}, bf16[256,128]{1,0:T(8,128)(2,1)S(1)}, u32[]{:S(2)}, u32[]{:S(2)}) collective-permute-start(bf16[256,128]{1,0:T(8,128)(2,1)S(1)} %get-tuple-element.44), channel_id=1, source_target_pairs={{0,16},{16,32},{32,48},{48,0},{64,80},{80,96},{96,112},{112,64},{1... | collective-permute-start | bytes 196616 | tf_op jit(solution)/shard_map/ppermute | solution.py:22
  65.5 7.2 %collective-permute-start.20 = (bf16[256,128]{1,0:T(8,128)(2,1)S(1)}, bf16[256,128]{1,0:T(8,128)(2,1)S(1)}, u32[]{:S(2)}, u32[]{:S(2)}) collective-permute-start(bf16[256,128]{1,0:T(8,128)(2,1)S(1)} %get-tuple-element.45), channel_id=1, source_target_pairs={{0,48},{16,0},{32,16},{48,32},{64,112},{80,64},{96,80},{112,96},{1... | collective-permute-start | bytes 196616 | tf_op jit(solution)/shard_map/ppermute | solution.py:22
  67.0 6.0 %collective-permute-start.25 = (bf16[256,128]{1,0:T(8,128)(2,1)S(1)}, bf16[256,128]{1,0:T(8,128)(2,1)S(1)}, u32[]{:S(2)}, u32[]{:S(2)}) collective-permute-start(bf16[256,128]{1,0:T(8,128)(2,1)S(1)} %get-tuple-element.46), channel_id=1, source_target_pairs={{0,128},{16,144},{32,160},{48,176},{64,192},{80,208},{96,224},{112... | collective-permute-start | bytes 196616 | tf_op jit(solution)/shard_map/ppermute | solution.py:22
  69.0 5.5 %collective-permute-start.27 = (bf16[256,128]{1,0:T(8,128)(2,1)S(1)}, bf16[256,128]{1,0:T(8,128)(2,1)S(1)}, u32[]{:S(2)}, u32[]{:S(2)}) collective-permute-start(bf16[256,128]{1,0:T(8,128)(2,1)S(1)} %get-tuple-element.47), channel_id=1, source_target_pairs={{0,64},{16,80},{32,96},{48,112},{64,128},{80,144},{96,160},{112,17... | collective-permute-start | bytes 196616 | tf_op jit(solution)/shard_map/ppermute | solution.py:22
  71.6 4.3 %collective-permute-start.26 = (bf16[256,128]{1,0:T(8,128)(2,1)S(1)}, bf16[256,128]{1,0:T(8,128)(2,1)S(1)}, u32[]{:S(2)}, u32[]{:S(2)}) collective-permute-start(bf16[256,128]{1,0:T(8,128)(2,1)S(1)} %get-tuple-element.48), channel_id=1, source_target_pairs={{0,192},{16,208},{32,224},{48,240},{64,0},{80,16},{96,32},{112,48}... | collective-permute-start | bytes 196616 | tf_op jit(solution)/shard_map/ppermute | solution.py:22
  76.3 5.6 %collective-permute-start.28 = (bf16[2,2,64,128]{3,0,2,1:T(2,128)(2,1)S(1)}, bf16[2,2,64,128]{3,0,2,1:T(2,128)(2,1)S(1)}, u32[]{:S(2)}, u32[]{:S(2)}) collective-permute-start(bf16[2,2,64,128]{3,0,2,1:T(2,128)(2,1)S(1)} %fusion.8), channel_id=1, source_target_pairs={{0,2},{1,3},{2,0},{3,1},{4,6},{5,7},{6,4},{7,5},{8,10},{9,11},{10,... | collective-permute-start | bytes 196616 | tf_op jit(solution)/shard_map/ppermute | solution.py:26
  (1 other events, 0.7 us)

commit v3 on v2

--- a/solution.py
+++ b/solution.py
@@ -324,8 +324,11 @@
     grads = jnp.stack([grad_0, grad_1]).reshape(heads, 2, 2, BLOCK // 4, head_dim)
     keep = jnp.where(lower, grads[:, :, 0], grads[:, :, 1])
     send = jnp.where(lower, grads[:, :, 1], grads[:, :, 0]).astype(low)
-    grads = (keep + swap(send, 2).astype(full)).transpose(1, 2, 0, 3)
-    return (query_grad, grads[0], grads[1])
+    far = swap(send, 2).astype(full)
+    key_grad, value_grad = (
+        jnp.stack([keep[a, n] + far[a, n] for a in range(heads)], axis=1) for n in range(2)
+    )
+    return (query_grad, key_grad, value_grad)
 
 
 def solution(mesh):

time: 84 us -> 89.6 us (1.067)
  the two profiles are of different devices: /device:TPU:0 before, /device:TPU:30 now
where the time goes in v3:
time: 89.6 us; the launch traced here: 89.4 us
  starting transfers between devices  37.1 us (41%)
  waiting for transfers between devices  28.6 us (32%)
  Pallas kernels  15.3 us (17%)
  other arithmetic  4.03 us (4%)
  local copies, waits for them, and re-layouts  3.48 us (4%)
  between operations  0.95 us (1%)
    ppermute x24, starting transfers between devices, move(): return lax.ppermute(array, 'ctx', shifts(rows, columns))  29.1 us
    ppermute x24, waiting for transfers between devices, move(): return lax.ppermute(array, 'ctx', shifts(rows, columns))  21.3 us
    pallas_call x3, Pallas kernels, attend_call(): pl.pallas_call(lambda *refs: attend(*refs, which=which, parts=parts, scal...  13.3 us
    ppermute x5, starting transfers between devices, swap(): return lax.ppermute(array, 'dp', [(d, d ^ bit) for d in range(4)])  7.97 us
    ppermute x5, waiting for transfers between devices, swap(): return lax.ppermute(array, 'dp', [(d, d ^ bit) for d in range(4)])  7.32 us
    pallas_call x1, Pallas kernels, plan_call(): pl.pallas_call(lambda *refs: plan(*refs, pairs=pairs), out_shape=[jax.Sha...  2.02 us
  transfers between devices with their start and end apart: 29, of which 11 were waited for; matrix products, arithmetic and copies ran while one was open for 5% of the time, Pallas kernels for 13%

profile of v3, /device:TPU:30, one launch (start us, length us, event | category | flops | bytes accessed | tf_op | source)
XLA Modules:
  0.0 89.4 jit_solution(12467859472392137643)
XLA Ops:
  1.5 3.4 %collective-permute-start.2 = (bf16[2,2,64,128]{3,2,1,0:T(8,128)(2,1)S(1)}, bf16[2,2,64,128]{3,2,1,0:T(8,128)(2,1)S(1)}, u32[]{:S(2)}, u32[]{:S(2)}) collective-permute-start(bf16[2,2,64,128]{3,2,1,0:T(8,128)(2,1)S(1)} %maximum_bitcast_fusion.1), channel_id=1, source_target_pairs={{0,2},{1,3},{2,0},{3,1},{4,6},{5,7},{6,4},{7,5},{8,10},{9,11},{10,... | collective-permute-start | bytes 196616 | tf_op jit(solution)/shard_map/ppermute | solution.py:26
  4.8 1.7 %maximum_bitcast_fusion = bf16[2,2,2,256,128]{4,2,1,3,0:T(2,128)(2,1)S(1)} fusion(bf16[1,256,2,2,128]{4,3,2,1,0:T(2,128)(2,1)S(1)} %bitcast.96, bf16[1,256,2,2,128]{4,3,2,1,0:T(2,128)(2,1)} %bitcast.99), kind=kLoop, calls=%fused_computation | loop fusion | flops 262144 | bytes 1048576 | tf_op jit(solution)/shard_map/transpose | solution.py:294
  6.7 2.0 %collective-permute-start.1 = (bf16[2,4,256,128]{3,2,1,0:T(8,128)(2,1)S(1)}, bf16[2,4,256,128]{3,2,1,0:T(8,128)(2,1)S(1)}, u32[]{:S(2)}, u32[]{:S(2)}) collective-permute-start(bf16[2,4,256,128]{3,2,1,0:T(8,128)(2,1)S(1)} %bitcast.89), channel_id=1, source_target_pairs={{0,1},{1,0},{2,3},{3,2},{4,5},{5,4},{6,7},{7,6},{8,9},{9,8},{10,11... | collective-permute-start | bytes 1572872 | tf_op jit(solution)/shard_map/ppermute | solution.py:26
  8.7 0.9 multiply_reduce_fusion
  11.3 0.9 %collective-permute-start.7 = (bf16[256,128]{1,0:T(8,128)(2,1)S(1)}, bf16[256,128]{1,0:T(8,128)(2,1)S(1)}, u32[]{:S(2)}, u32[]{:S(2)}) collective-permute-start(bf16[256,128]{1,0:T(8,128)(2,1)S(1)} %bitcast.105), channel_id=1, source_target_pairs={{0,128},{16,144},{32,160},{48,176},{64,192},{80,208},{96,224},{112... | collective-permute-start | bytes 196616 | tf_op jit(solution)/shard_map/ppermute | solution.py:22
  12.2 2.2 %collective-permute-start.6 = (bf16[256,128]{1,0:T(8,128)(2,1)S(1)}, bf16[256,128]{1,0:T(8,128)(2,1)S(1)}, u32[]{:S(2)}, u32[]{:S(2)}) collective-permute-start(bf16[256,128]{1,0:T(8,128)(2,1)S(1)} %bitcast.106), channel_id=1, source_target_pairs={{0,64},{16,80},{32,96},{48,112},{64,128},{80,144},{96,160},{112,17... | collective-permute-start | bytes 196616 | tf_op jit(solution)/shard_map/ppermute | solution.py:22
  14.4 0.8 collective-permute-start.5
  16.0 1.4 %collective-permute-start.4 = (bf16[256,128]{1,0:T(8,128)(2,1)S(1)}, bf16[256,128]{1,0:T(8,128)(2,1)S(1)}, u32[]{:S(2)}, u32[]{:S(2)}) collective-permute-start(bf16[256,128]{1,0:T(8,128)(2,1)S(1)} %bitcast.101), channel_id=1, source_target_pairs={{0,32},{16,48},{32,0},{48,16},{64,96},{80,112},{96,64},{112,80},{1... | collective-permute-start | bytes 196616 | tf_op jit(solution)/shard_map/ppermute | solution.py:22
  17.4 2.1 %collective-permute-start.3 = (bf16[256,128]{1,0:T(8,128)(2,1)S(1)}, bf16[256,128]{1,0:T(8,128)(2,1)S(1)}, u32[]{:S(2)}, u32[]{:S(2)}) collective-permute-start(bf16[256,128]{1,0:T(8,128)(2,1)S(1)} %bitcast.102), channel_id=1, source_target_pairs={{0,16},{16,32},{32,48},{48,0},{64,80},{80,96},{96,112},{112,64},{1... | collective-permute-start | bytes 196616 | tf_op jit(solution)/shard_map/ppermute | solution.py:22
  20.3 1.5 %collective-permute-done.4 = bf16[256,128]{1,0:T(8,128)(2,1)S(1)} collective-permute-done((bf16[256,128]{1,0:T(8,128)(2,1)S(1)}, bf16[256,128]{1,0:T(8,128)(2,1)S(1)}, u32[]{:S(2)}, u32[]{:S(2)}) %collective-permute-start.4) | collective-permute-done | bytes 65568 | tf_op jit(solution)/shard_map/ppermute | solution.py:22
  21.8 1.1 %collective-permute-done.3 = bf16[256,128]{1,0:T(8,128)(2,1)S(1)} collective-permute-done((bf16[256,128]{1,0:T(8,128)(2,1)S(1)}, bf16[256,128]{1,0:T(8,128)(2,1)S(1)}, u32[]{:S(2)}, u32[]{:S(2)}) %collective-permute-start.3) | collective-permute-done | bytes 65568 | tf_op jit(solution)/shard_map/ppermute | solution.py:22
  22.9 1.8 %collective-permute-start.9 = (bf16[4,256,128]{2,1,0:T(8,128)(2,1)S(1)}, bf16[4,256,128]{2,1,0:T(8,128)(2,1)S(1)}, u32[]{:S(2)}, u32[]{:S(2)}) collective-permute-start(bf16[4,256,128]{2,1,0:T(8,128)(2,1)S(1)} %pad_maximum_fusion.refs_4_), channel_id=1, source_target_pairs={{0,64},{16,80},{32,96},{48,112},{64,128},{80,144},{96,160},{112,17... | collective-permute-start | bytes 786440 | tf_op jit(solution)/shard_map/ppermute | solution.py:22
  26.4 2.1 %collective-permute-done = f32[3,4,256]{2,1,0:T(4,128)S(1)} collective-permute-done((f32[3,4,256]{2,1,0:T(4,128)S(1)}, f32[3,4,256]{2,1,0:T(4,128)S(1)}, u32[]{:S(2)}, u32[]{:S(2)}) %collective-permute-start) | collective-permute-done | bytes 12320 | tf_op jit(solution)/shard_map/ppermute | solution.py:26
  28.9 2.9 %collective-permute-start.12 = (bf16[4,256,128]{2,1,0:T(8,128)(2,1)S(1)}, bf16[4,256,128]{2,1,0:T(8,128)(2,1)S(1)}, u32[]{:S(2)}, u32[]{:S(2)}) collective-permute-start(bf16[4,256,128]{2,1,0:T(8,128)(2,1)S(1)} %collective-permute-done.11.refs_6_), channel_id=1, source_target_pairs={{0,16},{16,32},{32,48},{48,0},{64,80},{80,96},{96,112},{112,64},{1... | collective-permute-start | bytes 786440 | tf_op jit(solution)/shard_map/ppermute | solution.py:22
  31.8 1.9 %collective-permute-start.10 = (bf16[4,256,128]{2,1,0:T(8,128)(2,1)S(1)}, bf16[4,256,128]{2,1,0:T(8,128)(2,1)S(1)}, u32[]{:S(2)}, u32[]{:S(2)}) collective-permute-start(bf16[4,256,128]{2,1,0:T(8,128)(2,1)S(1)} %collective-permute-done.9.refs_4_), channel_id=1, source_target_pairs={{0,64},{16,80},{32,96},{48,112},{64,128},{80,144},{96,160},{112,17... | collective-permute-start | bytes 786440 | tf_op jit(solution)/shard_map/ppermute | solution.py:22
  33.7 2.0 %plan.1 = (s32[720]{0:T(1024)S(1)}, bf16[2,8,256,128]{3,2,1,0:T(8,128)(2,1)S(1)}) custom-call(s32[8,8]{1,0:T(8,128)S(1)} %fusion.13.refs_0_, s32[3]{0:T(128)S(1)} %pad_add_fusion.refs_1_, bf16[2,4,256,128]{3,2,1,0:T(8,128)(2,1)S(1)} %bitcast.90, bf16[2,4,256,128]{3,2,1,0:T(8,128)(2,1)S(1)} %collective-permute-done.1.refs_3_), custom_call_target="tpu_custom_call" | custom-call | flops 1048576 | bytes 4194304 | tf_op jit(solution)/shard_map/plan/pallas_call | solution.py:108
  36.1 5.6 %shard_map.94 = (bf16[4,256,128]{2,1,0:T(8,128)(2,1)S(1)}, bf16[4,256,128]{2,1,0:T(8,128)(2,1)S(1)}, bf16[4,256,128]{2,1,0:T(8,128)(2,1)S(1)}, bf16[4,256,128]{2,1,0:T(8,128)(2,1)S(1)}, f32[8,128,256]{2,1,0:T(8,128)S(1)}) custom-call(s32[720]{0:T(1024)S(1)} %get-tuple-element.21.refs_0_, s32[3]{0:T(128)S(1)} %pad_add_fusion.refs_1_, ...), custom_call_target="tpu_custom_call" | custom-call | flops 1342177280 | bytes 8388608 | tf_op jit(solution)/shard_map/pallas_call | solution.py:258
  41.7 3.5 %shard_map.95 = (bf16[4,256,128]{2,1,0:T(8,128)(2,1)S(1)}, bf16[4,256,128]{2,1,0:T(8,128)(2,1)S(1)}, f32[8,128,256]{2,1,0:T(8,128)S(1)}) custom-call(s32[720]{0:T(1024)S(1)} %get-tuple-element.21.refs_0_, s32[3]{0:T(128)S(1)} %pad_add_fusion.refs_1_, f32[16,256]{1,0:T(8,128)S(1)} %fusion.12.refs_2_, bf16[2,8,256,128]{3,2,1,0:T(8,128)(2,1)S(1)} %get-tuple-element.22.refs_3_, ...), custom_call_target="tpu_custom_call" | custom-call | flops 671088640 | bytes 6291456 | tf_op jit(solution)/shard_map/pallas_call | solution.py:258
  45.3 4.2 %shard_map.96 = (f32[4,256,128]{2,1,0:T(8,128)S(1)}, f32[4,256,128]{2,1,0:T(8,128)S(1)}, f32[4,256,128]{2,1,0:T(8,128)S(1)}, bf16[4,256,128]{2,1,0:T(8,128)(2,1)S(1)}) custom-call(s32[720]{0:T(1024)S(1)} %get-tuple-element.21.refs_0_, s32[3]{0:T(128)S(1)} %pad_add_fusion.refs_1_, f32[16,256]{1,0:T(8,128)S(1)} %fusion.12.refs_2_, ...), custom_call_target="tpu_custom_call" | custom-call | flops 671088640 | bytes 6291456 | tf_op jit(solution)/shard_map/pallas_call | solution.py:258
  50.3 3.2 %collective-permute-start.18 = (bf16[4,256,128]{2,1,0:T(8,128)(2,1)S(1)}, bf16[4,256,128]{2,1,0:T(8,128)(2,1)S(1)}, u32[]{:S(2)}, u32[]{:S(2)}) collective-permute-start(bf16[4,256,128]{2,1,0:T(8,128)(2,1)S(1)} %get-tuple-element.32), channel_id=1, source_target_pairs={{0,64},{16,80},{32,96},{48,112},{64,128},{80,144},{96,160},{112,17... | collective-permute-start | bytes 786440 | tf_op jit(solution)/shard_map/ppermute | solution.py:22
  53.5 0.8 collective-permute-start.24
  54.4 1.2 %collective-permute-start.22 = (bf16[4,256,128]{2,1,0:T(8,128)(2,1)S(1)}, bf16[4,256,128]{2,1,0:T(8,128)(2,1)S(1)}, u32[]{:S(2)}, u32[]{:S(2)}) collective-permute-start(bf16[4,256,128]{2,1,0:T(8,128)(2,1)S(1)} %get-tuple-element.33), channel_id=1, source_target_pairs={{0,48},{16,0},{32,16},{48,32},{64,112},{80,64},{96,80},{112,96},{1... | collective-permute-start | bytes 786440 | tf_op jit(solution)/shard_map/ppermute | solution.py:22
  56.0 1.0 %copy.48 = bf16[2,2,256,128]{3,1,0,2:T(2,128)(2,1)} copy(bf16[2,2,256,128]{3,2,1,0:T(8,128)(2,1)S(1)} %bitcast.97) | data formatting | bytes 524288 | tf_op jit(solution)/shard_map/reshape | solution.py:319
  57.0 8.1 %collective-permute-done.22 = bf16[4,256,128]{2,1,0:T(8,128)(2,1)S(1)} collective-permute-done((bf16[4,256,128]{2,1,0:T(8,128)(2,1)S(1)}, bf16[4,256,128]{2,1,0:T(8,128)(2,1)S(1)}, u32[]{:S(2)}, u32[]{:S(2)}) %collective-permute-start.22) | collective-permute-done | bytes 262176 | tf_op jit(solution)/shard_map/ppermute | solution.py:22
  65.4 1.1 %collective-permute-start.19 = (bf16[256,128]{1,0:T(8,128)(2,1)S(1)}, bf16[256,128]{1,0:T(8,128)(2,1)S(1)}, u32[]{:S(2)}, u32[]{:S(2)}) collective-permute-start(bf16[256,128]{1,0:T(8,128)(2,1)S(1)} %get-tuple-element.59), channel_id=1, source_target_pairs={{0,32},{16,48},{32,0},{48,16},{64,96},{80,112},{96,64},{112,80},{1... | collective-permute-start | bytes 196616 | tf_op jit(solution)/shard_map/ppermute | solution.py:22
  66.5 2.3 %collective-permute-start.21 = (bf16[256,128]{1,0:T(8,128)(2,1)S(1)}, bf16[256,128]{1,0:T(8,128)(2,1)S(1)}, u32[]{:S(2)}, u32[]{:S(2)}) collective-permute-start(bf16[256,128]{1,0:T(8,128)(2,1)S(1)} %get-tuple-element.60), channel_id=1, source_target_pairs={{0,16},{16,32},{32,48},{48,0},{64,80},{80,96},{96,112},{112,64},{1... | collective-permute-start | bytes 196616 | tf_op jit(solution)/shard_map/ppermute | solution.py:22
  69.6 4.0 %collective-permute-done.23 = bf16[4,256,128]{2,1,0:T(8,128)(2,1)S(1)} collective-permute-done((bf16[4,256,128]{2,1,0:T(8,128)(2,1)S(1)}, bf16[4,256,128]{2,1,0:T(8,128)(2,1)S(1)}, u32[]{:S(2)}, u32[]{:S(2)}) %collective-permute-start.23) | collective-permute-done | bytes 262176 | tf_op jit(solution)/shard_map/ppermute | solution.py:22
  73.8 2.7 %collective-permute-start.27 = (bf16[256,128]{1,0:T(8,128)(2,1)S(1)}, bf16[256,128]{1,0:T(8,128)(2,1)S(1)}, u32[]{:S(2)}, u32[]{:S(2)}) collective-permute-start(bf16[256,128]{1,0:T(8,128)(2,1)S(1)} %get-tuple-element.63), channel_id=1, source_target_pairs={{0,64},{16,80},{32,96},{48,112},{64,128},{80,144},{96,160},{112,17... | collective-permute-start | bytes 196616 | tf_op jit(solution)/shard_map/ppermute | solution.py:22
  76.5 3.0 %collective-permute-done.25 = bf16[256,128]{1,0:T(8,128)(2,1)S(1)} collective-permute-done((bf16[256,128]{1,0:T(8,128)(2,1)S(1)}, bf16[256,128]{1,0:T(8,128)(2,1)S(1)}, u32[]{:S(2)}, u32[]{:S(2)}) %collective-permute-start.25) | collective-permute-done | bytes 65568 | tf_op jit(solution)/shard_map/ppermute | solution.py:22
  79.5 2.4 %collective-permute-done.26 = bf16[256,128]{1,0:T(8,128)(2,1)S(1)} collective-permute-done((bf16[256,128]{1,0:T(8,128)(2,1)S(1)}, bf16[256,128]{1,0:T(8,128)(2,1)S(1)}, u32[]{:S(2)}, u32[]{:S(2)}) %collective-permute-start.26) | collective-permute-done | bytes 65568 | tf_op jit(solution)/shard_map/ppermute | solution.py:22
  82.0 1.0 %collective-permute-start.28 = (bf16[2,2,64,128]{3,2,1,0:T(8,128)(2,1)S(1)}, bf16[2,2,64,128]{3,2,1,0:T(8,128)(2,1)S(1)}, u32[]{:S(2)}, u32[]{:S(2)}) collective-permute-start(bf16[2,2,64,128]{3,2,1,0:T(8,128)(2,1)S(1)} %fusion.9), channel_id=1, source_target_pairs={{0,2},{1,3},{2,0},{3,1},{4,6},{5,7},{6,4},{7,5},{8,10},{9,11},{10,... | collective-permute-start | bytes 196616 | tf_op jit(solution)/shard_map/ppermute | solution.py:26
  83.0 5.0 %collective-permute-done.28 = bf16[2,2,64,128]{3,2,1,0:T(8,128)(2,1)S(1)} collective-permute-done((bf16[2,2,64,128]{3,2,1,0:T(8,128)(2,1)S(1)}, bf16[2,2,64,128]{3,2,1,0:T(8,128)(2,1)S(1)}, u32[]{:S(2)}, u32[]{:S(2)}) %collective-permute-start.28) | collective-permute-done | bytes 65568 | tf_op jit(solution)/shard_map/ppermute | solution.py:26
  (76 shorter events, 10.7 us)
Async XLA Ops:
  0.6 4.2 %copy-start = (bf16[256,2,2,128]{3,2,1,0:T(2,128)(2,1)S(1)}, bf16[256,2,2,128]{3,2,1,0:T(2,128)(2,1)}, u32[]{:S(2)}) copy-start(bf16[256,2,2,128]{3,2,1,0:T(2,128)(2,1)} %param.11) | copy-start | bytes 786436
  1.5 8.9 %collective-permute-start.2 = (bf16[2,2,64,128]{3,2,1,0:T(8,128)(2,1)S(1)}, bf16[2,2,64,128]{3,2,1,0:T(8,128)(2,1)S(1)}, u32[]{:S(2)}, u32[]{:S(2)}) collective-permute-start(bf16[2,2,64,128]{3,2,1,0:T(8,128)(2,1)S(1)} %maximum_bitcast_fusion.1), channel_id=1, source_target_pairs={{0,2},{1,3},{2,0},{3,1},{4,6},{5,7},{6,4},{7,5},{8,10},{9,11},{10,... | collective-permute-start | bytes 196616 | tf_op jit(solution)/shard_map/ppermute | solution.py:26
  6.6 2.1 %copy-start.3 = (s32[1,2,2,8]{3,2,1,0:T(2,128)S(1)}, s32[1,2,2,8]{3,2,1,0:T(2,128)}, u32[]{:S(2)}) copy-start(s32[1,2,2,8]{3,2,1,0:T(2,128)} %param.13) | copy-start | bytes 388
  6.6 2.1 %copy-start.1 = (bf16[256,2,2,128]{3,2,1,0:T(2,128)(2,1)S(1)}, bf16[256,2,2,128]{3,2,1,0:T(2,128)(2,1)}, u32[]{:S(2)}) copy-start(bf16[256,2,2,128]{3,2,1,0:T(2,128)(2,1)} %param.10) | copy-start | bytes 786436
  6.7 27.0 %collective-permute-start.1 = (bf16[2,4,256,128]{3,2,1,0:T(8,128)(2,1)S(1)}, bf16[2,4,256,128]{3,2,1,0:T(8,128)(2,1)S(1)}, u32[]{:S(2)}, u32[]{:S(2)}) collective-permute-start(bf16[2,4,256,128]{3,2,1,0:T(8,128)(2,1)S(1)} %bitcast.89), channel_id=1, source_target_pairs={{0,1},{1,0},{2,3},{3,2},{4,5},{5,4},{6,7},{7,6},{8,9},{9,8},{10,11... | collective-permute-start | bytes 1572872 | tf_op jit(solution)/shard_map/ppermute | solution.py:26
  10.5 5.6 %collective-permute-start.8 = (bf16[256,128]{1,0:T(8,128)(2,1)S(1)}, bf16[256,128]{1,0:T(8,128)(2,1)S(1)}, u32[]{:S(2)}, u32[]{:S(2)}) collective-permute-start(bf16[256,128]{1,0:T(8,128)(2,1)S(1)} %bitcast.104), channel_id=1, source_target_pairs={{0,192},{16,208},{32,224},{48,240},{64,0},{80,16},{96,32},{112,48}... | collective-permute-start | bytes 196616 | tf_op jit(solution)/shard_map/ppermute | solution.py:22
  11.3 6.1 %collective-permute-start.7 = (bf16[256,128]{1,0:T(8,128)(2,1)S(1)}, bf16[256,128]{1,0:T(8,128)(2,1)S(1)}, u32[]{:S(2)}, u32[]{:S(2)}) collective-permute-start(bf16[256,128]{1,0:T(8,128)(2,1)S(1)} %bitcast.105), channel_id=1, source_target_pairs={{0,128},{16,144},{32,160},{48,176},{64,192},{80,208},{96,224},{112... | collective-permute-start | bytes 196616 | tf_op jit(solution)/shard_map/ppermute | solution.py:22
  12.2 7.3 %collective-permute-start.6 = (bf16[256,128]{1,0:T(8,128)(2,1)S(1)}, bf16[256,128]{1,0:T(8,128)(2,1)S(1)}, u32[]{:S(2)}, u32[]{:S(2)}) collective-permute-start(bf16[256,128]{1,0:T(8,128)(2,1)S(1)} %bitcast.106), channel_id=1, source_target_pairs={{0,64},{16,80},{32,96},{48,112},{64,128},{80,144},{96,160},{112,17... | collective-permute-start | bytes 196616 | tf_op jit(solution)/shard_map/ppermute | solution.py:22
  14.4 5.8 %collective-permute-start.5 = (bf16[256,128]{1,0:T(8,128)(2,1)S(1)}, bf16[256,128]{1,0:T(8,128)(2,1)S(1)}, u32[]{:S(2)}, u32[]{:S(2)}) collective-permute-start(bf16[256,128]{1,0:T(8,128)(2,1)S(1)} %bitcast.100), channel_id=1, source_target_pairs={{0,48},{16,0},{32,16},{48,32},{64,112},{80,64},{96,80},{112,96},{1... | collective-permute-start | bytes 196616 | tf_op jit(solution)/shard_map/ppermute | solution.py:22
  16.0 5.8 %collective-permute-start.4 = (bf16[256,128]{1,0:T(8,128)(2,1)S(1)}, bf16[256,128]{1,0:T(8,128)(2,1)S(1)}, u32[]{:S(2)}, u32[]{:S(2)}) collective-permute-start(bf16[256,128]{1,0:T(8,128)(2,1)S(1)} %bitcast.101), channel_id=1, source_target_pairs={{0,32},{16,48},{32,0},{48,16},{64,96},{80,112},{96,64},{112,80},{1... | collective-permute-start | bytes 196616 | tf_op jit(solution)/shard_map/ppermute | solution.py:22
  17.4 5.4 %collective-permute-start.3 = (bf16[256,128]{1,0:T(8,128)(2,1)S(1)}, bf16[256,128]{1,0:T(8,128)(2,1)S(1)}, u32[]{:S(2)}, u32[]{:S(2)}) collective-permute-start(bf16[256,128]{1,0:T(8,128)(2,1)S(1)} %bitcast.102), channel_id=1, source_target_pairs={{0,16},{16,32},{32,48},{48,0},{64,80},{80,96},{96,112},{112,64},{1... | collective-permute-start | bytes 196616 | tf_op jit(solution)/shard_map/ppermute | solution.py:22
  19.6 9.3 %collective-permute-start.11 = (bf16[4,256,128]{2,1,0:T(8,128)(2,1)S(1)}, bf16[4,256,128]{2,1,0:T(8,128)(2,1)S(1)}, u32[]{:S(2)}, u32[]{:S(2)}) collective-permute-start(bf16[4,256,128]{2,1,0:T(8,128)(2,1)S(1)} %pad_maximum_fusion.1.refs_5_), channel_id=1, source_target_pairs={{0,16},{16,32},{32,48},{48,0},{64,80},{80,96},{96,112},{112,64},{1... | collective-permute-start | bytes 786440 | tf_op jit(solution)/shard_map/ppermute | solution.py:22
  22.9 8.9 %collective-permute-start.9 = (bf16[4,256,128]{2,1,0:T(8,128)(2,1)S(1)}, bf16[4,256,128]{2,1,0:T(8,128)(2,1)S(1)}, u32[]{:S(2)}, u32[]{:S(2)}) collective-permute-start(bf16[4,256,128]{2,1,0:T(8,128)(2,1)S(1)} %pad_maximum_fusion.refs_4_), channel_id=1, source_target_pairs={{0,64},{16,80},{32,96},{48,112},{64,128},{80,144},{96,160},{112,17... | collective-permute-start | bytes 786440 | tf_op jit(solution)/shard_map/ppermute | solution.py:22
  24.7 3.8 %collective-permute-start = (f32[3,4,256]{2,1,0:T(4,128)S(1)}, f32[3,4,256]{2,1,0:T(4,128)S(1)}, u32[]{:S(2)}, u32[]{:S(2)}) collective-permute-start(f32[3,4,256]{2,1,0:T(4,128)S(1)} %constant_dynamic-update-slice_fusion), channel_id=1, source_target_pairs={{0,1},{1,0},{2,3},{3,2},{4,5},{5,4},{6,7},{7,6},{8,9},{9,8},{10,11... | collective-permute-start | bytes 36872 | tf_op jit(solution)/shard_map/ppermute | solution.py:26
  25.5 10.2 %collective-permute-start.14 = (bf16[4,256,128]{2,1,0:T(8,128)(2,1)S(1)}, bf16[4,256,128]{2,1,0:T(8,128)(2,1)S(1)}, u32[]{:S(2)}, u32[]{:S(2)}) collective-permute-start(bf16[4,256,128]{2,1,0:T(8,128)(2,1)S(1)} %pad_maximum_fusion.1.refs_5_), channel_id=1, source_target_pairs={{0,48},{16,0},{32,16},{48,32},{64,112},{80,64},{96,80},{112,96},{1... | collective-permute-start | bytes 786440 | tf_op jit(solution)/shard_map/ppermute | solution.py:22
  28.5 7.6 %collective-permute-start.13 = (bf16[4,256,128]{2,1,0:T(8,128)(2,1)S(1)}, bf16[4,256,128]{2,1,0:T(8,128)(2,1)S(1)}, u32[]{:S(2)}, u32[]{:S(2)}) collective-permute-start(bf16[4,256,128]{2,1,0:T(8,128)(2,1)S(1)} %pad_maximum_fusion.refs_4_), channel_id=1, source_target_pairs={{0,192},{16,208},{32,224},{48,240},{64,0},{80,16},{96,32},{112,48}... | collective-permute-start | bytes 786440 | tf_op jit(solution)/shard_map/ppermute | solution.py:22
  28.9 12.8 %collective-permute-start.12 = (bf16[4,256,128]{2,1,0:T(8,128)(2,1)S(1)}, bf16[4,256,128]{2,1,0:T(8,128)(2,1)S(1)}, u32[]{:S(2)}, u32[]{:S(2)}) collective-permute-start(bf16[4,256,128]{2,1,0:T(8,128)(2,1)S(1)} %collective-permute-done.11.refs_6_), channel_id=1, source_target_pairs={{0,16},{16,32},{32,48},{48,0},{64,80},{80,96},{96,112},{112,64},{1... | collective-permute-start | bytes 786440 | tf_op jit(solution)/shard_map/ppermute | solution.py:22
  31.8 9.9 %collective-permute-start.10 = (bf16[4,256,128]{2,1,0:T(8,128)(2,1)S(1)}, bf16[4,256,128]{2,1,0:T(8,128)(2,1)S(1)}, u32[]{:S(2)}, u32[]{:S(2)}) collective-permute-start(bf16[4,256,128]{2,1,0:T(8,128)(2,1)S(1)} %collective-permute-done.9.refs_4_), channel_id=1, source_target_pairs={{0,64},{16,80},{32,96},{48,112},{64,128},{80,144},{96,160},{112,17... | collective-permute-start | bytes 786440 | tf_op jit(solution)/shard_map/ppermute | solution.py:22
  45.2 10.4 %collective-permute-start.16 = (bf16[4,256,128]{2,1,0:T(8,128)(2,1)S(1)}, bf16[4,256,128]{2,1,0:T(8,128)(2,1)S(1)}, u32[]{:S(2)}, u32[]{:S(2)}) collective-permute-start(bf16[4,256,128]{2,1,0:T(8,128)(2,1)S(1)} %get-tuple-element.27), channel_id=1, source_target_pairs={{0,192},{16,208},{32,224},{48,240},{64,0},{80,16},{96,32},{112,48}... | collective-permute-start | bytes 786440 | tf_op jit(solution)/shard_map/ppermute | solution.py:22
  49.5 6.5 %collective-permute-start.15 = (bf16[4,256,128]{2,1,0:T(8,128)(2,1)S(1)}, bf16[4,256,128]{2,1,0:T(8,128)(2,1)S(1)}, u32[]{:S(2)}, u32[]{:S(2)}) collective-permute-start(bf16[4,256,128]{2,1,0:T(8,128)(2,1)S(1)} %get-tuple-element.26), channel_id=1, source_target_pairs={{0,1},{1,0},{2,3},{3,2},{4,5},{5,4},{6,7},{7,6},{8,9},{9,8},{10,11... | collective-permute-start | bytes 786440 | tf_op jit(solution)/shard_map/ppermute | solution.py:26
  50.3 14.9 %collective-permute-start.18 = (bf16[4,256,128]{2,1,0:T(8,128)(2,1)S(1)}, bf16[4,256,128]{2,1,0:T(8,128)(2,1)S(1)}, u32[]{:S(2)}, u32[]{:S(2)}) collective-permute-start(bf16[4,256,128]{2,1,0:T(8,128)(2,1)S(1)} %get-tuple-element.32), channel_id=1, source_target_pairs={{0,64},{16,80},{32,96},{48,112},{64,128},{80,144},{96,160},{112,17... | collective-permute-start | bytes 786440 | tf_op jit(solution)/shard_map/ppermute | solution.py:22
  53.5 16.0 %collective-permute-start.24 = (bf16[4,256,128]{2,1,0:T(8,128)(2,1)S(1)}, bf16[4,256,128]{2,1,0:T(8,128)(2,1)S(1)}, u32[]{:S(2)}, u32[]{:S(2)}) collective-permute-start(bf16[4,256,128]{2,1,0:T(8,128)(2,1)S(1)} %get-tuple-element.38), channel_id=1, source_target_pairs={{0,16},{16,32},{32,48},{48,0},{64,80},{80,96},{96,112},{112,64},{1... | collective-permute-start | bytes 786440 | tf_op jit(solution)/shard_map/ppermute | solution.py:22
  54.4 10.7 %collective-permute-start.22 = (bf16[4,256,128]{2,1,0:T(8,128)(2,1)S(1)}, bf16[4,256,128]{2,1,0:T(8,128)(2,1)S(1)}, u32[]{:S(2)}, u32[]{:S(2)}) collective-permute-start(bf16[4,256,128]{2,1,0:T(8,128)(2,1)S(1)} %get-tuple-element.33), channel_id=1, source_target_pairs={{0,48},{16,0},{32,16},{48,32},{64,112},{80,64},{96,80},{112,96},{1... | collective-permute-start | bytes 786440 | tf_op jit(solution)/shard_map/ppermute | solution.py:22
  55.6 9.6 %collective-permute-start.17 = (bf16[4,256,128]{2,1,0:T(8,128)(2,1)S(1)}, bf16[4,256,128]{2,1,0:T(8,128)(2,1)S(1)}, u32[]{:S(2)}, u32[]{:S(2)}) collective-permute-start(bf16[4,256,128]{2,1,0:T(8,128)(2,1)S(1)} %add_convert_fusion.1), channel_id=1, source_target_pairs={{0,192},{16,208},{32,224},{48,240},{64,0},{80,16},{96,32},{112,48}... | collective-permute-start | bytes 786440 | tf_op jit(solution)/shard_map/ppermute | solution.py:22
  65.2 8.4 %collective-permute-start.23 = (bf16[4,256,128]{2,1,0:T(8,128)(2,1)S(1)}, bf16[4,256,128]{2,1,0:T(8,128)(2,1)S(1)}, u32[]{:S(2)}, u32[]{:S(2)}) collective-permute-start(bf16[4,256,128]{2,1,0:T(8,128)(2,1)S(1)} %add_convert_fusion), channel_id=1, source_target_pairs={{0,48},{16,0},{32,16},{48,32},{64,112},{80,64},{96,80},{112,96},{1... | collective-permute-start | bytes 786440 | tf_op jit(solution)/shard_map/ppermute | solution.py:22
  65.4 11.1 %collective-permute-start.19 = (bf16[256,128]{1,0:T(8,128)(2,1)S(1)}, bf16[256,128]{1,0:T(8,128)(2,1)S(1)}, u32[]{:S(2)}, u32[]{:S(2)}) collective-permute-start(bf16[256,128]{1,0:T(8,128)(2,1)S(1)} %get-tuple-element.59), channel_id=1, source_target_pairs={{0,32},{16,48},{32,0},{48,16},{64,96},{80,112},{96,64},{112,80},{1... | collective-permute-start | bytes 196616 | tf_op jit(solution)/shard_map/ppermute | solution.py:22
  66.5 10.0 %collective-permute-start.21 = (bf16[256,128]{1,0:T(8,128)(2,1)S(1)}, bf16[256,128]{1,0:T(8,128)(2,1)S(1)}, u32[]{:S(2)}, u32[]{:S(2)}) collective-permute-start(bf16[256,128]{1,0:T(8,128)(2,1)S(1)} %get-tuple-element.60), channel_id=1, source_target_pairs={{0,16},{16,32},{32,48},{48,0},{64,80},{80,96},{96,112},{112,64},{1... | collective-permute-start | bytes 196616 | tf_op jit(solution)/shard_map/ppermute | solution.py:22
  68.8 7.7 %collective-permute-start.20 = (bf16[256,128]{1,0:T(8,128)(2,1)S(1)}, bf16[256,128]{1,0:T(8,128)(2,1)S(1)}, u32[]{:S(2)}, u32[]{:S(2)}) collective-permute-start(bf16[256,128]{1,0:T(8,128)(2,1)S(1)} %get-tuple-element.61), channel_id=1, source_target_pairs={{0,48},{16,0},{32,16},{48,32},{64,112},{80,64},{96,80},{112,96},{1... | collective-permute-start | bytes 196616 | tf_op jit(solution)/shard_map/ppermute | solution.py:22
  73.7 5.9 %collective-permute-start.25 = (bf16[256,128]{1,0:T(8,128)(2,1)S(1)}, bf16[256,128]{1,0:T(8,128)(2,1)S(1)}, u32[]{:S(2)}, u32[]{:S(2)}) collective-permute-start(bf16[256,128]{1,0:T(8,128)(2,1)S(1)} %get-tuple-element.62), channel_id=1, source_target_pairs={{0,128},{16,144},{32,160},{48,176},{64,192},{80,208},{96,224},{112... | collective-permute-start | bytes 196616 | tf_op jit(solution)/shard_map/ppermute | solution.py:22
  73.8 5.8 %collective-permute-start.27 = (bf16[256,128]{1,0:T(8,128)(2,1)S(1)}, bf16[256,128]{1,0:T(8,128)(2,1)S(1)}, u32[]{:S(2)}, u32[]{:S(2)}) collective-permute-start(bf16[256,128]{1,0:T(8,128)(2,1)S(1)} %get-tuple-element.63), channel_id=1, source_target_pairs={{0,64},{16,80},{32,96},{48,112},{64,128},{80,144},{96,160},{112,17... | collective-permute-start | bytes 196616 | tf_op jit(solution)/shard_map/ppermute | solution.py:22
  76.5 5.5 %collective-permute-start.26 = (bf16[256,128]{1,0:T(8,128)(2,1)S(1)}, bf16[256,128]{1,0:T(8,128)(2,1)S(1)}, u32[]{:S(2)}, u32[]{:S(2)}) collective-permute-start(bf16[256,128]{1,0:T(8,128)(2,1)S(1)} %get-tuple-element.64), channel_id=1, source_target_pairs={{0,192},{16,208},{32,224},{48,240},{64,0},{80,16},{96,32},{112,48}... | collective-permute-start | bytes 196616 | tf_op jit(solution)/shard_map/ppermute | solution.py:22
  82.0 6.0 %collective-permute-start.28 = (bf16[2,2,64,128]{3,2,1,0:T(8,128)(2,1)S(1)}, bf16[2,2,64,128]{3,2,1,0:T(8,128)(2,1)S(1)}, u32[]{:S(2)}, u32[]{:S(2)}) collective-permute-start(bf16[2,2,64,128]{3,2,1,0:T(8,128)(2,1)S(1)} %fusion.9), channel_id=1, source_target_pairs={{0,2},{1,3},{2,0},{3,1},{4,6},{5,7},{6,4},{7,5},{8,10},{9,11},{10,... | collective-permute-start | bytes 196616 | tf_op jit(solution)/shard_map/ppermute | solution.py:26
  (1 other events, 0.7 us)
